TPU v7x, 512 devices: a whole 4x8x8 slice. The times are simulated.
512 devices in a mesh: dp: 32 (over y, x), group: 16 (over z, core).
Axes of the slice: x: 4, y: 8, z: 8, core: 2. Of those that a mesh axis runs over, the one named last changes fastest.
Arguments:
- tokens: bfloat16 [163840, 768], P(('dp', 'group')), may hold values from -6 to 6
- cotangent: bfloat16 [163840, 768], P(('dp', 'group')), may hold values from -18 to 18
- patch_mask: int32 [163840], P(('dp', 'group')), may hold values 0 or 1
- image_tiles: int32 [512, 3], replicated, may hold values from 0 to 9, as said below
- patches: int32 [512, 3], replicated, may hold values from 0 to 288, as said below
- w_in: bfloat16 [288, 384], replicated, may hold values from -0.375 to 0.375
- b_in: float32 [384], replicated, may hold values from -1 to 1
- w_out: bfloat16 [384, 288], replicated, may hold values from -0.3125 to 0.3125
- ln_gain: float32 [768], replicated, may hold values from 0.5 to 1.5
- ln_shift: float32 [768], replicated, may hold values from -0.5 to 0.5
Outputs:
- dtokens: bfloat16 [163840, 768], P(('dp', 'group'))
- grad_w_in: bfloat16 [288, 384], replicated
- grad_b_in: bfloat16 [384], replicated
- grad_w_out: bfloat16 [384, 288], replicated
- grad_b_out: bfloat16 [288], replicated
- grad_gain: bfloat16 [768], replicated
- grad_shift: bfloat16 [768], replicated
Inputs may be any that keep to these rules, and one draw needn't show every extreme that they name: `image_tiles`: entry s of row d is the number of tiles of the s-th image slot of device row d, 0 for an empty slot. A device's tiles sum to at most 10, reached on some device. . An image has at most 9 tiles, reached in every draw. For an image of k tiles, patches lies between max(32, 32 * (k - 1) + 1) and 32 * k; it is 0 for an empty slot.
All inputs are finite; a program needn't handle non-finite values. No bound on the sum of `patch_mask` on one device may be relied on, other than what follows from the above.
Results may differ from a plain program's by a relative error of at most 0.0085.
Values may be sent and summed in bfloat16 or wider, within the bound.
A program may use at most 64 MiB of HBM per device.

v0:
```python
import math

import jax
import jax.numpy as jnp
from jax import lax
from jax.sharding import Mesh
from jax.sharding import PartitionSpec as P

PMAX = 288
TILE = 32
DP_GROUP = ("dp_0", "dp_1", "group_0", "group_1")


highest = lax.Precision.HIGHEST
ln_epsilon = 1e-05
clip_share = 0.5


def rows_for(lines, peers):
    spare = -len(lines) % peers
    return jnp.pad(lines, [(0, spare)] + [(0, 0)] * (lines.ndim - 1))


def copy_for_each(value, axis):
    peers = lax.axis_size(axis)
    return lax.all_to_all(
        jnp.broadcast_to(value[None], (peers, *value.shape)), axis, 0, 0, tiled=True
    )


def in_order(blocks, dim):
    blocks = jnp.moveaxis(blocks, 0, dim)
    shape = blocks.shape
    return blocks.reshape(*shape[:dim], shape[dim] * shape[dim + 1], *shape[dim + 2 :])


def whole_of(value, axes, dim):
    far, near = axes
    first = copy_for_each(value, far)
    blocks = jnp.swapaxes(copy_for_each(first, near), 0, 1)
    return in_order(blocks.reshape(-1, *value.shape), dim)


def in_blocks(value, dim, peers):
    shape = value.shape
    blocks = value.reshape(*shape[:dim], peers, shape[dim] // peers, *shape[dim + 1 :])
    return jnp.moveaxis(blocks, dim, 0)


def sum_at_owner(value, axis, dim):
    peers = lax.axis_size(axis)
    blocks = lax.all_to_all(in_blocks(value, dim, peers), axis, 0, 0, tiled=True)
    return jnp.sum(blocks, axis=0)


def sum_in_two_steps(value, axes, dim):
    far, near = axes
    own = sum_at_owner(in_blocks(value, dim, lax.axis_size(far)), near, dim + 1)
    return jnp.sum(lax.all_to_all(own, far, 0, 0, tiled=True), axis=0)


def nested_sum(value, axes):
    padded = rows_for(value, lax.axis_size(axes[0]) * lax.axis_size(axes[1]))
    whole = whole_of(sum_in_two_steps(padded, axes, 0), axes, 0)
    return lax.slice_in_dim(whole, 0, len(value)).reshape(value.shape)


def together(arrays, axis):
    ends = [0]
    for a in arrays:
        ends.append(ends[-1] + a.size)
    subtotal = nested_sum(jnp.concatenate([a.ravel() for a in arrays]), axis)
    return tuple((subtotal[b:e].reshape(a.shape) for a, b, e in zip(arrays, ends, ends[1:])))


def gelu_pair(preact):
    normal_cdf = 0.5 * (1.0 + lax.erf(preact * 0.7071067811865476))
    density = jnp.exp(-0.5 * preact * preact) * 0.3989422804014327
    return (preact * normal_cdf, normal_cdf + preact * density)


def tile_layout(tile_rows, tile_total):
    starts = jnp.cumsum(tile_rows, axis=1) - tile_rows
    places = jnp.arange(tile_total, dtype=jnp.int32)
    inside = (places[None, :, None] >= starts[:, None, :]) & (
        places[None, :, None] < (starts + tile_rows)[:, None, :]
    )
    offset = places[None, :, None] - starts[:, None, :]
    return (inside, offset)


def tile_tables(inside, offset, spans):
    img_hot = inside.astype(jnp.float32)
    tile_alive = jnp.sum(inside.astype(jnp.int32), axis=1)
    span_index = jnp.sum(jnp.where(inside, offset, 0), axis=1)
    span_hot = (
        (span_index[:, None] == jnp.arange(spans, dtype=jnp.int32)[None, :])
        & (tile_alive[:, None] > 0)
    ).astype(jnp.float32)
    image_index = jnp.sum(
        jnp.where(inside, jnp.arange(inside.shape[1], dtype=jnp.int32)[None, :], 0), axis=1
    )
    return (img_hot, span_hot, image_index)


def image_core(normed, dout, inside_tiles, span_hot, w_in, b_in, w_out):
    tile_total, slots = inside_tiles.shape
    spans = span_hot.shape[1]
    hidden = w_in.shape[1]
    tile_len = w_in.shape[0] // spans
    rows, width = normed.shape
    span_bf = span_hot.astype(jnp.bfloat16)
    rows_in = jnp.dot(
        span_bf, w_in.reshape(spans, tile_len * hidden), preferred_element_type=jnp.float32
    )
    rows_in = rows_in.astype(jnp.bfloat16).reshape(rows, hidden)
    cols_out = jnp.einsum(
        "tj,hjp->tph",
        span_bf,
        w_out.reshape(hidden, spans, tile_len),
        preferred_element_type=jnp.float32,
    )
    cols_out = cols_out.astype(jnp.bfloat16).reshape(rows, hidden)
    row_hot = (
        jnp.broadcast_to(inside_tiles[:, None, :], (tile_total, tile_len, slots))
        .reshape(rows, slots)
        .astype(jnp.bfloat16)
    )
    in_wide = (rows_in[:, None, :] * row_hot[:, :, None]).reshape(rows, slots * hidden)
    out_wide = (cols_out[:, None, :] * row_hot[:, :, None]).reshape(rows, slots * hidden)
    preact = (
        jnp.einsum("rc,rk->ck", normed, in_wide, preferred_element_type=jnp.float32).reshape(
            width, slots, hidden
        )
        + b_in
    )
    dz_all = jnp.einsum("rc,rk->ck", dout, out_wide, preferred_element_type=jnp.float32).reshape(
        width, slots, hidden
    )
    act, slope = gelu_pair(preact)
    act_b = act.astype(jnp.bfloat16).reshape(width, slots * hidden)
    dpre = dz_all * slope
    dpre_b = dpre.astype(jnp.bfloat16).reshape(width, slots * hidden)
    grad_b_in = jnp.sum(dpre, axis=(0, 1))
    row_mask = row_hot.astype(jnp.float32)[:, :, None]
    grad_rows_in = jnp.sum(
        jnp.einsum("rc,ck->rk", normed, dpre_b, preferred_element_type=jnp.float32).reshape(
            rows, slots, hidden
        )
        * row_mask,
        axis=1,
    )
    grad_rows_out = jnp.sum(
        jnp.einsum("rc,ck->rk", dout, act_b, preferred_element_type=jnp.float32).reshape(
            rows, slots, hidden
        )
        * row_mask,
        axis=1,
    )
    grad_w_in = jnp.einsum(
        "tj,tph->jph",
        span_hot,
        grad_rows_in.reshape(tile_total, tile_len, hidden),
        precision=highest,
    ).reshape(spans * tile_len, hidden)
    grad_w_out = jnp.einsum(
        "tj,tph->hjp",
        span_hot,
        grad_rows_out.reshape(tile_total, tile_len, hidden),
        precision=highest,
    ).reshape(hidden, spans * tile_len)
    out_sums = jnp.sum(dout.astype(jnp.float32), axis=1).reshape(tile_total, tile_len)
    grad_b_out = jnp.einsum("tj,tp->jp", span_hot, out_sums, precision=highest).reshape(-1)
    dnormed = jnp.einsum("rk,ck->rc", in_wide, dpre_b, preferred_element_type=jnp.float32).astype(
        jnp.bfloat16
    )
    return ((grad_w_in, grad_b_in, grad_w_out, grad_b_out), dnormed)


def clip_factor(total, entry_count):
    return jnp.minimum(1.0, clip_share * math.sqrt(entry_count) / jnp.sqrt(total + 1e-06))


def local(
    tokens, cotangent, patch_mask, image_tiles, patches, w_in, b_in, w_out, ln_gain, ln_shift
):
    tile_len = TILE
    spans = PMAX // TILE
    tile_total = tokens.shape[0] // tile_len
    me_index = lax.axis_index(DP_GROUP)
    own_tiles = lax.dynamic_slice_in_dim(image_tiles, me_index, 1, 0)
    own_patches = lax.dynamic_slice_in_dim(patches, me_index, 1, 0)
    inside, offset = tile_layout(own_tiles, tile_total)
    row_place = offset[..., None] * tile_len + jnp.arange(tile_len, dtype=jnp.int32)
    alive = jnp.sum(
        (inside[..., None] & (row_place < own_patches[:, None, :, None])).astype(jnp.int32), axis=2
    ).reshape(-1)
    alive_rows = (alive * patch_mask).astype(jnp.float32)
    values = tokens.astype(jnp.float32)
    center = values - jnp.mean(values, axis=1, keepdims=True)
    inv_std = lax.rsqrt(jnp.mean(center * center, axis=1, keepdims=True) + ln_epsilon)
    normal_x = center * inv_std
    normed = ((normal_x * ln_gain + ln_shift) * alive_rows[:, None]).astype(jnp.bfloat16)
    dout = (cotangent.astype(jnp.float32) * alive_rows[:, None]).astype(jnp.bfloat16)
    img_hot, span_hot, image_index = tile_tables(inside[0], offset[0], spans)
    terms, dnormed = image_core(normed, dout, inside[0], span_hot, w_in, b_in, w_out)
    d_rows = dnormed.astype(jnp.float32) * alive_rows[:, None]
    grad_gain = jnp.sum(d_rows * normal_x, axis=0)
    grad_shift = jnp.sum(d_rows, axis=0)
    scaled = d_rows * ln_gain
    inner = jnp.mean(scaled * normal_x, axis=1, keepdims=True)
    d_norm = (scaled - jnp.mean(scaled, axis=1, keepdims=True) - normal_x * inner) * inv_std
    dtokens = (cotangent.astype(jnp.float32) + d_norm).astype(jnp.bfloat16)
    grad_w_in, grad_b_in, grad_w_out, grad_b_out = terms
    pieces = (grad_w_in, grad_b_in, grad_w_out, grad_b_out, grad_gain, grad_shift)
    entry_count = sum((piece.size for piece in pieces))
    summed = together(
        (grad_w_in, grad_b_in, grad_w_out, grad_b_out, grad_gain, grad_shift),
        ("dp_0", ("dp_1", "group_0", "group_1")),
    )
    total = sum((jnp.sum(piece * piece) for piece in summed))
    factor = clip_factor(total, entry_count)
    results = [(piece * factor).astype(jnp.bfloat16) for piece in summed]
    return (dtokens, results[0], results[1], results[2], results[3], results[4], results[5])


def solution(mesh):
    finer = Mesh(mesh.devices.reshape(8, 4, 8, 2), ("dp_0", "dp_1", "group_0", "group_1"))
    in_specs = (
        P(DP_GROUP, None),
        P(DP_GROUP, None),
        P(DP_GROUP),
        P(),
        P(),
        P(),
        P(),
        P(),
        P(),
        P(),
    )
    out_specs = (P(DP_GROUP, None), P(), P(), P(), P(), P(), P())
    return jax.shard_map(local, mesh=finer, in_specs=in_specs, out_specs=out_specs, check_vma=False)
```

profile of v0, /device:TPU:1, one launch (start us, length us, event | category | flops | bytes accessed | tf_op | source)
XLA Modules:
  0.0 148.3 jit_solution(6052255661932353575)
XLA Ops:
  0.7 1.0 dynamic-slice_reduce_fusion
  2.1 1.2 convert_reduce_fusion
  3.3 1.3 fusion.33
  5.7 1.1 reshape.296
  7.6 1.3 fusion.36
  8.9 1.3 multiply_reduce_fusion
  10.3 3.1 %fusion.80 = (f32[384]{0:T(512)S(1)}, bf16[768,3,384]{0,2,1:T(8,128)(2,1)S(1)}) fusion(f32[768,3,384]{0,2,1:T(8,128)S(1)} %fusion.36, f32[384]{0:T(512)S(1)} %copy-done.6, bf16[320,384]{0,1:T(8,128)(2,1)S(1)} %copy.79, bf16[320,3]{0,1:T(4,128)(2,1)S(1)} %convert_element_type.116, f32[320]{0:T(512)S(1)} %multiply_convert_fusion.7, ...), kind=kOutput, calls=%fused_computation.112 | convolution fusion | flops 579059328 | bytes 6051968 | tf_op jit(solution)/shard_map/rc,rk->ck/dot_general | solution.py:137
  13.4 1.0 multiply_reduce_fusion.1
  14.3 1.2 fusion.32
  15.5 1.7 %convolution_bitcast_fusion.1 = f32[384,9,32]{0,1,2:T(8,128)} fusion(f32[10,32,384]{2,1,0:T(8,128)S(1)} %bitcast.82, s32[10]{0:T(128)S(1)} %get-tuple-element.46, pred[10]{0:T(512)(128)(4,1)S(1)} %broadcast_compare_fusion), kind=kOutput, calls=%fused_computation.17 | convolution fusion | flops 13271220 | bytes 933938 | tf_op jit(solution)/shard_map/tj,tph->hjp/dot_general | solution.py:166
  17.3 1.3 convert_reduce_fusion.1
  18.9 0.8 fusion.42
  19.8 0.8 reshape_reshape.12
  20.6 2.2 %copy.87 = f32[384,9,32]{2,1,0:T(8,128)S(1)} copy(f32[384,9,32]{0,1,2:T(8,128)} %convolution_bitcast_fusion.1) | data formatting | bytes 884736 | tf_op jit(solution)/shard_map/tj,tph->hjp/transpose | solution.py:166
  22.8 1.4 reshape_reshape.13
  24.2 7.9 %concatenate.3 = f32[223392]{0:T(1024)S(1)} concatenate(f32[110592]{0:T(1024)} %reshape_reshape.12, f32[384]{0:T(512)S(1)} %get-tuple-element.56, f32[110592]{0:T(1024)} %reshape_reshape.13, f32[288]{0:T(512)S(1)} %reshape.304, f32[768]{0:T(1024)S(1)} %get-tuple-element.35, f32[768]{0:T(1024)S(1)} %get-tuple-element.38), dimensions={0} | concatenate | bytes 1787136 | tf_op jit(solution)/shard_map/concatenate | solution.py:72
  32.2 0.8 reshape_reshape.14
  33.6 43.1 %all_to_all.25 = f32[64,8,437]{2,1,0:T(8,128)S(1)} all-to-all(f32[64,8,437]{2,1,0:T(8,128)S(1)} %copy.88), channel_id=1, replica_groups=mesh['dp_0'=8,'dp_1'=4,'group_0'=8,'group_1'=2] {'dp_1','group_0','group..., dimensions={0} | all-to-all | bytes 1789952 | tf_op jit(solution)/shard_map/all_to_all | solution.py:52
  76.8 13.2 %all_to_all.26 = f32[8,1,437]{2,1,0:T(1,128)S(1)} all-to-all(f32[8,1,437]{2,1,0:T(1,128)S(1)} %all_to_all.17), channel_id=1, replica_groups=mesh['dp_0'=8,'dp_1'=4,'group_0'=8,'group_1'=2] {'dp_0'}, dimensions={0} | all-to-all | bytes 27968 | tf_op jit(solution)/shard_map/all_to_all | solution.py:59
  90.1 9.0 %all_to_all.27 = f32[8,1,437]{2,1,0:T(1,128)S(1)} all-to-all(f32[8,1,437]{2,1,0:T(1,128)S(1)} %broadcast_in_dim.13), channel_id=1, replica_groups=mesh['dp_0'=8,'dp_1'=4,'group_0'=8,'group_1'=2] {'dp_0'}, dimensions={0} | all-to-all | bytes 27968 | tf_op jit(solution)/shard_map/all_to_all | solution.py:26
  99.2 37.1 %all_to_all.28 = f32[64,8,437]{2,1,0:T(8,128)S(1)} all-to-all(f32[64,8,437]{2,1,0:T(8,128)S(1)} %broadcast_in_dim.15), channel_id=1, replica_groups=mesh['dp_0'=8,'dp_1'=4,'group_0'=8,'group_1'=2] {'dp_1','group_0','group..., dimensions={0} | all-to-all | bytes 1789952 | tf_op jit(solution)/shard_map/all_to_all | solution.py:26
  137.0 0.9 reshape_reshape.15
  146.7 0.8 copy.90
  147.5 0.8 convert_element_type.132
  (59 shorter events, 9.1 us)
Async XLA Ops:
  0.6 4.5 %copy-start = (bf16[384,288]{0,1:T(8,128)(2,1)S(1)}, bf16[384,288]{0,1:T(8,128)(2,1)}, u32[]{:S(2)}) copy-start(bf16[384,288]{0,1:T(8,128)(2,1)} %param.17) | copy-start | bytes 663556
  0.6 6.9 %copy-start.1 = (bf16[320,768]{1,0:T(8,128)(2,1)S(1)}, bf16[320,768]{1,0:T(8,128)(2,1)}, u32[]{:S(2)}) copy-start(bf16[320,768]{1,0:T(8,128)(2,1)} %param.10) | copy-start | bytes 1474564
  0.7 6.9 %copy-start.5 = (s32[320]{0:T(512)S(1)}, s32[320]{0:T(512)}, u32[]{:S(2)}) copy-start(s32[320]{0:T(512)} %param.12) | copy-start | bytes 3844
  0.7 6.9 %copy-start.3 = (f32[768]{0:T(1024)S(1)}, f32[768]{0:T(1024)}, u32[]{:S(2)}) copy-start(f32[768]{0:T(1024)} %param.18) | copy-start | bytes 9220
  0.7 6.9 %copy-start.4 = (f32[768]{0:T(1024)S(1)}, f32[768]{0:T(1024)}, u32[]{:S(2)}) copy-start(f32[768]{0:T(1024)} %param.19) | copy-start | bytes 9220
  5.7 3.2 %copy-start.2 = (bf16[320,768]{1,0:T(8,128)(2,1)S(1)}, bf16[320,768]{1,0:T(8,128)(2,1)}, u32[]{:S(2)}) copy-start(bf16[320,768]{1,0:T(8,128)(2,1)} %param.11) | copy-start | bytes 1474564
  5.7 3.2 %copy-start.6 = (f32[384]{0:T(512)S(1)}, f32[384]{0:T(512)}, u32[]{:S(2)}) copy-start(f32[384]{0:T(512)} %param.16) | copy-start | bytes 4612
where the time goes:
time: 149 us; the launch traced here: 148 us
  blocking collectives  102 us (68%)
  local copies, waits for them, and re-layouts  20.9 us (14%)
  matrix products  11.1 us (7%)
  other arithmetic  8.93 us (6%)
  between operations  4.87 us (3%)
    all_to_all x2, blocking collectives, copy_for_each(): lax.all_to_all(jnp.broadcast_to(value[None], (peers, *value.shape)), axis...  46.1 us
    all_to_all x1, blocking collectives, sum_at_owner(): lax.all_to_all(in_blocks(value, dim, peers), axis, 0, 0, tiled=True)  43.1 us
    all_to_all x1, blocking collectives, sum_in_two_steps(): return jnp.sum(lax.all_to_all(own, far, 0, 0, tiled=True), axis=0)  13.2 us
    concatenate x1, local copies, waits for them, and re-layouts, together(): subtotal = nested_sum(jnp.concatenate([a.ravel() for a in arrays]), axis)  7.91 us
    dot_general x1, matrix products, image_core(): jnp.einsum('rc,rk->ck', dout, out_wide, preferred_element_type=jnp.float32)  3.07 us

commit v1 on v0

v1 whole, which is shorter than its diff:
```python
import math

import jax
import jax.numpy as jnp
from jax import lax
from jax.experimental import pallas as pl
from jax.experimental.pallas import tpu as pltpu
from jax.sharding import PartitionSpec as P

PMAX = 288
TILE = 32
TILES = 10
ROWS = TILE * TILES
C = 768
H = 384
NX = 4
SPANS = (288, 160, 96)
BASES = (0, 288, 448)
PAD_ROWS = ROWS + PMAX
LINES = 16
BLOCKS = 64
ENTRIES = 2 * PMAX * H + H + PMAX + 2 * C

ln_epsilon = 1e-05
clip_share = 0.5
F32 = jnp.float32
BF16 = jnp.bfloat16
MESH = pl.DeviceIdType.MESH
AXES = ("dp", "group")
VMEM = pl.BlockSpec(memory_space=pltpu.VMEM)
SMEM = pl.BlockSpec(memory_space=pltpu.SMEM)


def dot(a, b, da, db):
    return lax.dot_general(a, b, (((da,), (db,)), ((), ())), preferred_element_type=F32)


def gelu_pair(preact):
    normal_cdf = 0.5 * (1.0 + lax.erf(preact * 0.7071067811865476))
    density = jnp.exp(-0.5 * preact * preact) * 0.3989422804014327
    return (preact * normal_cdf, normal_cdf + preact * density)


def wide(col):
    return jnp.concatenate([col] * (C // 128), axis=1)


def column(row):
    return jnp.transpose(jnp.broadcast_to(row, (128, row.shape[1])))


def image_table(tiles_ref, patches_ref, place):
    tiles = [tiles_ref[s, place] for s in range(3)]
    counts = [patches_ref[s, place] for s in range(3)]
    starts = [jnp.int32(0), tiles[0], tiles[0] + tiles[1]]
    images = list(zip(tiles, starts, counts))
    for i, j in ((0, 1), (0, 2), (1, 2)):
        a, b = images[i], images[j]
        swap = b[0] > a[0]
        images[i] = tuple(jnp.where(swap, q, p) for p, q in zip(a, b))
        images[j] = tuple(jnp.where(swap, p, q) for p, q in zip(a, b))
    return images


def compute_kernel(
    tiles_ref, patches_ref, tok_ref, cot_ref, mask_ref, wi_ref, bi_ref, wo_ref, gain_ref, shift_ref,
    dtok_ref, pack_ref,
    nx_ref, inv_ref, alive_ref, x_ref, d_ref, dn_ref, act_ref, dpre_ref, gi_ref, go_ref, bo_ref, small_ref,
):
    place = lax.axis_index("dp") * lax.axis_size("group") + lax.axis_index("group")
    images = image_table(tiles_ref, patches_ref, place)
    row = lax.broadcasted_iota(jnp.int32, (ROWS, 128), 0)
    alive = jnp.zeros((ROWS, 128), F32)
    for _, start, count in images:
        first = start * TILE
        alive = jnp.where((row >= first) & (row < first + count), 1.0, alive)
    alive_ref[...] = alive * column(mask_ref[...].astype(F32))
    gain = gain_ref[...]
    shift = shift_ref[...]
    x_ref[ROWS:, :] = jnp.zeros((PMAX, C), BF16)
    d_ref[ROWS:, :] = jnp.zeros((PMAX, C), BF16)
    for t in range(TILES):
        rows = slice(t * TILE, (t + 1) * TILE)
        live = wide(alive_ref[rows, :])
        values = tok_ref[rows, :].astype(F32)
        center = values - jnp.mean(values, axis=1, keepdims=True)
        inv = lax.rsqrt(jnp.mean(center * center, axis=1, keepdims=True) + ln_epsilon)
        normal = center * inv
        nx_ref[rows, :] = normal
        inv_ref[rows, :] = jnp.broadcast_to(inv, (TILE, 128))
        x_ref[rows, :] = ((normal * gain + shift) * live).astype(BF16)
        d_ref[rows, :] = (cot_ref[rows, :].astype(F32) * live).astype(BF16)

    bias = column(bi_ref[...])
    ones = jnp.ones((16, C), BF16)
    bo_ref[...] = jnp.zeros((16, H), F32)
    sums = [jnp.zeros((128, 128), F32) for _ in range(3)]
    for j, (tiles, start, _) in enumerate(images):
        span = SPANS[j]
        first = pl.multiple_of(start * TILE, TILE)
        inside = lax.broadcasted_iota(jnp.int32, (span, 128), 0) < tiles * TILE
        inside = wide(inside.astype(F32).astype(BF16))
        xs = x_ref[pl.ds(first, span), :] * inside
        ds = d_ref[pl.ds(first, span), :] * inside
        for h in range(3):
            lines = slice(h * 128, (h + 1) * 128)
            preact = dot(wi_ref[:span, lines], xs, 0, 0) + wide(bias[lines, :])
            dz = dot(wo_ref[:span, lines], ds, 0, 0)
            act, slope = gelu_pair(preact)
            act_ref[lines, :] = act.astype(BF16)
            dpre = dz * slope
            dpre_ref[lines, :] = dpre.astype(BF16)
            for b in range(C // 128):
                sums[h] = sums[h] + dpre[:, b * 128 : (b + 1) * 128]
        gi = dot(xs, dpre_ref[...], 1, 1)
        go = dot(ds, act_ref[...], 1, 1)
        bo = dot(ones, ds, 1, 1)
        if j == 0:
            gi_ref[...] = gi
            go_ref[...] = go
            bo_ref[:, :span] = bo
        else:
            gi_ref[:span, :] += gi
            go_ref[:span, :] += go
            bo_ref[:, :span] += bo
        dn_ref[BASES[j] : BASES[j] + span, :] = dot(wi_ref[:span, :], dpre_ref[...], 1, 0).astype(BF16)

    gain_sum = jnp.zeros((8, C), F32)
    shift_sum = jnp.zeros((8, C), F32)
    for t in range(TILES):
        rows = slice(t * TILE, (t + 1) * TILE)
        source = jnp.int32(0)
        for j, (tiles, start, _) in enumerate(images):
            held = (start <= t) & (t < start + tiles)
            source = jnp.where(held, BASES[j] + (t - start) * TILE, source)
        source = pl.multiple_of(source, TILE)
        normal = nx_ref[rows, :]
        d_rows = dn_ref[pl.ds(source, TILE), :].astype(F32) * wide(alive_ref[rows, :])
        weighted = d_rows * normal
        for i in range(0, TILE, 8):
            gain_sum = gain_sum + weighted[i : i + 8]
            shift_sum = shift_sum + d_rows[i : i + 8]
        scaled = d_rows * gain
        inner = jnp.mean(scaled * normal, axis=1, keepdims=True)
        d_norm = (scaled - jnp.mean(scaled, axis=1, keepdims=True) - normal * inner) * wide(inv_ref[rows, :])
        dtok_ref[rows, :] = (cot_ref[rows, :].astype(F32) + d_norm).astype(BF16)

    small_ref[...] = jnp.zeros((2 * LINES, 128), F32)
    gain_row = jnp.sum(gain_sum, axis=0, keepdims=True)
    shift_row = jnp.sum(shift_sum, axis=0, keepdims=True)
    for b in range(6):
        small_ref[b : b + 1, :] = gain_row[:, b * 128 : (b + 1) * 128]
        small_ref[6 + b : 7 + b, :] = shift_row[:, b * 128 : (b + 1) * 128]
    for b in range(3):
        small_ref[16 + b : 17 + b, :] = jnp.sum(jnp.transpose(sums[b]), axis=0, keepdims=True)
        small_ref[19 + b : 20 + b, :] = bo_ref[0:1, b * 128 : (b + 1) * 128]
    for i in range(PMAX // LINES):
        for b in range(3):
            box = (slice(i * LINES, (i + 1) * LINES), slice(b * 128, (b + 1) * 128))
            pack_ref[0, i * 3 + b] = gi_ref[box].astype(BF16)
            pack_ref[1, i * 3 + b] = go_ref[box].astype(BF16)
    pack_ref[0, 54] = small_ref[:LINES, :].astype(BF16)
    pack_ref[0, 55] = small_ref[LINES:, :].astype(BF16)
    pack_ref[0, 56:] = jnp.zeros((8, LINES, 128), BF16)
    pack_ref[1, 54:] = jnp.zeros((10, LINES, 128), BF16)


def ring_order(n):
    order = []
    for d in range(1, n // 2 + 1):
        order.append(d)
        if n - d != d:
            order.append(n - d)
    return order


def copy_to(source, target, sems, device):
    send, recv = sems
    copy = pltpu.make_async_remote_copy(
        src_ref=source, dst_ref=target, send_sem=send, recv_sem=recv, device_id=device, device_id_type=MESH
    )
    copy.start()
    return copy


def comm_kernel(
    nx, ny, nz,
    pack_ref, out_ref,
    r0, q, r1, t_ref, r2, u_ref, r3,
    s0, v0, s1, v1, s2, v2, s3, v3, s4, v4, s5, v5, s6, v6,
):
    dp = lax.axis_index("dp")
    group = lax.axis_index("group")
    y, x = dp // nx, lax.rem(dp, nx)
    z, c = group // 2, lax.rem(group, 2)
    mate = 1 - c
    chip = (nz, ny)
    mine = (z, y)
    partner = (dp, z * 2 + mate)

    def z_peer(d):
        return (dp, lax.rem(z + d, nz) * 2 + c)

    def y_peer(d):
        return (lax.rem(y + d, ny) * nx + x, group)

    def x_peer(d):
        return (y * nx + lax.rem(x + d, nx), group)

    peers = (z_peer, y_peer)
    barrier = pltpu.get_barrier_semaphore()
    everyone = [partner]
    everyone += [z_peer(d) for d in range(1, nz)]
    everyone += [y_peer(d) for d in range(1, ny)]
    everyone += [x_peer(d) for d in range(1, nx)]
    for device in everyone:
        pl.semaphore_signal(barrier, inc=1, device_id=device, device_id_type=MESH)
    pl.semaphore_wait(barrier, len(everyone))
    copies = []

    first = {}
    orders = [list(reversed(ring_order(n))) + [0] for n in chip]
    for step in range(max(chip)):
        for k in (0, 1):
            if step < chip[k]:
                d = orders[k][step]
                at = lax.rem(mine[k] + d, chip[k])
                first[k, d] = copy_to(
                    pack_ref.at[k, mate, at], r0.at[k, at], (s0.at[k, d], v0.at[k, d]), partner
                )
                copies.append(first[k, d])
    second = {}
    for step in range(max(chip)):
        for k in (0, 1):
            if step < chip[k]:
                d = orders[k][step]
                at = lax.rem(mine[k] + d, chip[k])
                first[k, d].wait_recv()
                q[k, at] = (pack_ref[k, c, at].astype(F32) + r0[k, at].astype(F32)).astype(BF16)
                if d:
                    second[k, d] = copy_to(
                        q.at[k, at], r1.at[k, mine[k]], (s1.at[k, d], v1.at[k, d]), peers[k](d)
                    )
                    copies.append(second[k, d])
    for k in (0, 1):
        total = q[k, mine[k]].astype(F32)
        for d in ring_order(chip[k]):
            second[k, d].wait_recv()
            total = total + r1[k, lax.rem(mine[k] - d + chip[k], chip[k])].astype(F32)
        t_ref[:, k] = total.astype(BF16)
    third = {}
    for d in reversed(ring_order(nx)):
        third[d] = copy_to(t_ref.at[lax.rem(x + d, nx)], r2.at[x], (s2.at[d], v2.at[d]), x_peer(d))
        copies.append(third[d])
    total = t_ref[x].astype(F32)
    for d in ring_order(nx):
        third[d].wait_recv()
        total = total + r2[lax.rem(x - d + nx, nx)].astype(F32)
    u_ref[...] = total.astype(BF16)
    fourth = {}
    for k in (0, 1):
        n = chip[1 - k]
        for d in reversed(ring_order(n)):
            fourth[k, d] = copy_to(
                u_ref.at[k], r3.at[k, mine[1 - k]], (s3.at[k, d], v3.at[k, d]), peers[1 - k](d)
            )
            copies.append(fourth[k, d])
        r3[k, mine[1 - k]] = u_ref[k]
    fifth = {}
    for k in (0, 1):
        n = chip[1 - k]
        for d in ring_order(n):
            fourth[k, d].wait_recv()
        total = r3[k, 0].astype(F32)
        for i in range(1, n):
            total = total + r3[k, i].astype(F32)
        out_ref[k, c, mine[k], x] = total.astype(BF16)
        block = out_ref.at[k, c, mine[k], x]
        for d in reversed(ring_order(nx)):
            fifth[k, d] = copy_to(block, block, (s4.at[k, d], v4.at[k, d]), x_peer(d))
            copies.append(fifth[k, d])
    sixth = {}
    last = {}
    for k in (0, 1):
        for d in ring_order(nx):
            fifth[k, d].wait_recv()
        block = out_ref.at[k, c, mine[k]]
        for d in reversed(ring_order(chip[k])):
            sixth[k, d] = copy_to(block, block, (s5.at[k, d], v5.at[k, d]), peers[k](d))
            copies.append(sixth[k, d])
        last[k, 0] = copy_to(block, block, (s6.at[k, 0], v6.at[k, 0]), partner)
        copies.append(last[k, 0])
    orders = [ring_order(n) for n in chip]
    for step in range(max(chip) - 1):
        for k in (0, 1):
            if step < chip[k] - 1:
                d = orders[k][step]
                sixth[k, d].wait_recv()
                block = out_ref.at[k, c, lax.rem(mine[k] - d + chip[k], chip[k])]
                last[k, d] = copy_to(block, block, (s6.at[k, d], v6.at[k, d]), partner)
                copies.append(last[k, d])
    for copy in last.values():
        copy.wait_recv()
    for copy in copies:
        copy.wait_send()


def finish_kernel(sum_ref, wi_ref, bi_ref, wo_ref, bo_ref, gain_ref, shift_ref):
    total = jnp.zeros((LINES, 128), F32)
    for k in (0, 1):
        for i in range(56 - 2 * k):
            piece = sum_ref[k, i].astype(F32)
            total = total + piece * piece
    total = jnp.sum(jnp.sum(total, axis=1, keepdims=True), axis=0, keepdims=True)
    factor = jnp.minimum(1.0, clip_share * math.sqrt(ENTRIES) / jnp.sqrt(total + 1e-06))
    for i in range(PMAX // LINES):
        for b in range(3):
            box = (slice(i * LINES, (i + 1) * LINES), slice(b * 128, (b + 1) * 128))
            wi_ref[box] = (sum_ref[0, i * 3 + b].astype(F32) * factor).astype(BF16)
            wo_ref[box] = (sum_ref[1, i * 3 + b].astype(F32) * factor).astype(BF16)
    one = sum_ref[0, 54].astype(F32) * factor
    two = sum_ref[0, 55].astype(F32) * factor
    for b in range(6):
        at = slice(b * 128, (b + 1) * 128)
        gain_ref[:, at] = one[b : b + 1].astype(BF16)
        shift_ref[:, at] = one[6 + b : 7 + b].astype(BF16)
    for b in range(3):
        at = slice(b * 128, (b + 1) * 128)
        bi_ref[:, at] = two[b : b + 1].astype(BF16)
        bo_ref[:, at] = two[3 + b : 4 + b].astype(BF16)


def compute(tokens, cotangent, patch_mask, image_tiles, patches, w_in, b_in, w_out, ln_gain, ln_shift):
    shape = jax.ShapeDtypeStruct
    return pl.pallas_call(
        compute_kernel,
        name="compute",
        out_shape=(shape((ROWS, C), BF16), shape((2, BLOCKS, LINES, 128), BF16)),
        in_specs=[SMEM, SMEM] + [VMEM] * 8,
        out_specs=(VMEM, VMEM),
        scratch_shapes=[
            pltpu.VMEM((ROWS, C), F32),
            pltpu.VMEM((ROWS, 128), F32),
            pltpu.VMEM((ROWS, 128), F32),
            pltpu.VMEM((PAD_ROWS, C), BF16),
            pltpu.VMEM((PAD_ROWS, C), BF16),
            pltpu.VMEM((sum(SPANS), C), BF16),
            pltpu.VMEM((H, C), BF16),
            pltpu.VMEM((H, C), BF16),
            pltpu.VMEM((PMAX, H), F32),
            pltpu.VMEM((PMAX, H), F32),
            pltpu.VMEM((16, H), F32),
            pltpu.VMEM((2 * LINES, 128), F32),
        ],
    )(
        image_tiles.T, patches.T, tokens, cotangent, patch_mask.reshape(1, ROWS), w_in,
        b_in.reshape(1, H), w_out.T, ln_gain.reshape(1, C), ln_shift.reshape(1, C),
    )


def total_of(packed, nx, ny, nz):
    n = max(ny, nz)
    dma = pltpu.SemaphoreType.DMA
    block = (LINES, 128)
    sems = [(2, n), (2, n), (nx,), (2, n), (2, nx), (2, n), (2, n)]
    return pl.pallas_call(
        lambda *refs: comm_kernel(nx, ny, nz, *refs),
        name="exchange",
        out_shape=jax.ShapeDtypeStruct((2, 2, n, nx, *block), BF16),
        in_specs=[VMEM],
        out_specs=VMEM,
        scratch_shapes=[
            pltpu.VMEM((2, n, nx, *block), BF16),
            pltpu.VMEM((2, n, nx, *block), BF16),
            pltpu.VMEM((2, n, nx, *block), BF16),
            pltpu.VMEM((nx, 2, *block), BF16),
            pltpu.VMEM((nx, 2, *block), BF16),
            pltpu.VMEM((2, *block), BF16),
            pltpu.VMEM((2, n, *block), BF16),
        ]
        + [dma(shape) for shape in sems for _ in range(2)],
        compiler_params=pltpu.CompilerParams(collective_id=0, has_side_effects=True),
    )(packed.reshape(2, 2, n, nx, *block))


def finish(sums):
    shape = jax.ShapeDtypeStruct
    shapes = ((PMAX, H), (1, H), (PMAX, H), (1, H), (1, C), (1, C))
    return pl.pallas_call(
        finish_kernel,
        name="finish",
        out_shape=tuple(shape(s, BF16) for s in shapes),
        in_specs=[VMEM],
        out_specs=(VMEM,) * 6,
    )(sums)


def solution(mesh):
    ny, nz = mesh.shape["dp"] // NX, mesh.shape["group"] // 2

    def local(*args):
        dtokens, packed = compute(*args)
        sums = total_of(packed, NX, ny, nz).reshape(2, BLOCKS, LINES, 128)
        w_in, b_in, w_out, b_out, gain, shift = finish(sums)
        return (
            dtokens, w_in, b_in.reshape(H), w_out.T, b_out.reshape(H)[:PMAX], gain.reshape(C), shift.reshape(C)
        )

    rows = P(AXES, None)
    in_specs = (rows, rows, P(AXES)) + (P(),) * 7
    out_specs = (rows,) + (P(),) * 6
    return jax.shard_map(local, mesh=mesh, in_specs=in_specs, out_specs=out_specs, check_vma=False)
```

time: 149 us -> 60.2 us (0.40)
  blocking collectives: 102 us -> 0 us
  Pallas kernels: 0 us -> 53 us
  local copies, waits for them, and re-layouts: 20.9 us -> 4.4 us
  matrix products: 11.1 us -> 0 us
  other arithmetic: 8.93 us -> 1.77 us
  between operations: 4.87 us -> 0.68 us
    all_to_all x4 -> x0, blocking collectives: 102 us -> none  [the longest x2 46.1 us: copy_for_each(): lax.all_to_all(jnp.broadcast_to(value[None], (peers, *value.shape)), axis...]
    pallas_call x0 -> x3, Pallas kernels: none -> 53 us  [the longest x1 43.5 us: total_of(): pl.pallas_call(lambda *refs: comm_kernel(nx, ny, nz, *refs), name='exchan...]
    dot_general x10 -> x0, matrix products: 11.1 us -> none  [the longest x1 3.07 us: image_core(): jnp.einsum('rc,rk->ck', dout, out_wide, preferred_element_type=jnp.float32)]
    concatenate x1 -> x0, local copies, waits for them, and re-layouts: 7.91 us -> none  [together(): subtotal = nested_sum(jnp.concatenate([a.ravel() for a in arrays]), axis)]
    reduce_sum x11 -> x0, other arithmetic: 6.84 us -> none  [the longest x4 2.63 us: local(): total = sum((jnp.sum(piece * piece) for piece in summed))]
    another operation x4 -> x0, local copies, waits for them, and re-layouts: 3.79 us -> none  [the longest x2 2.13 us: together(): subtotal = nested_sum(jnp.concatenate([a.ravel() for a in arrays]), axis)]
    transpose x3 -> x0, local copies, waits for them, and re-layouts: 3.45 us -> none  [the longest x1 2.23 us: image_core(): jnp.einsum('tj,tph->hjp', span_hot, grad_rows_out.reshape(tile_total, til...]
    convert_element_type x7 -> x0, other arithmetic: 1.88 us -> none  [the longest x4 1.86 us: local(): results = [(piece * factor).astype(jnp.bfloat16) for piece in summed]]
where the time goes in v1:
time: 60.2 us; the launch traced here: 59.8 us
  Pallas kernels  53 us (88%)
  local copies, waits for them, and re-layouts  4.4 us (7%)
  other arithmetic  1.77 us (3%)
  between operations  0.68 us (1%)
    pallas_call x1, Pallas kernels, total_of(): pl.pallas_call(lambda *refs: comm_kernel(nx, ny, nz, *refs), name='exchan...  43.5 us
    pallas_call x1, Pallas kernels, compute(): pl.pallas_call(compute_kernel, name='compute', out_shape=(shape((ROWS, C)...  7.5 us
    pallas_call x1, Pallas kernels, finish(): pl.pallas_call(finish_kernel, name='finish', out_shape=tuple((shape(s, BF...  2.02 us
    pallas_call x3, other arithmetic, finish(): pl.pallas_call(finish_kernel, name='finish', out_shape=tuple((shape(s, BF...  1.77 us
    unnamed x16, local copies, waits for them, and re-layouts  1.53 us

profile of v1, /device:TPU:1, one launch (start us, length us, event | category | flops | bytes accessed | tf_op | source)
XLA Modules:
  0.0 59.8 jit_solution(15359104309607902738)
XLA Ops:
  0.6 0.0 copy-start.4
  0.6 0.0 copy-start.5
  0.7 0.0 copy-start
  0.7 0.7 %copy-done.4 = s32[320]{0:T(512)S(1)} copy-done((s32[320]{0:T(512)S(1)}, s32[320]{0:T(512)}, u32[]{:S(2)}) %copy-start.4) | copy-done | bytes 1304
  1.3 0.6 reshape.43.mask_ref
  1.9 0.0 copy-done.5
  1.9 0.6 reshape.44.bi_ref
  2.4 0.0 copy-done
  2.4 0.0 copy-start.1
  2.5 0.6 reshape.45.gain_ref
  3.0 0.1 copy-done.1
  3.1 0.6 reshape.46.shift_ref
  3.7 7.5 %compute.1 = (bf16[320,768]{1,0:T(8,128)(2,1)}, bf16[2,64,16,128]{3,2,1,0:T(8,128)(2,1)}) custom-call(s32[3,512]{1,0:T(4,128)} %bitcast.9, s32[3,512]{1,0:T(4,128)} %bitcast.10, bf16[320,768]{1,0:T(8,128)(2,1)} %tok_ref.1, bf16[320,768]{1,0:T(8,128)(2,1)} %cot_ref.1, s32[1,320]{1,0:T(1,128)} %reshape.43.mask_ref, bf16[288,384]{1,0:T(8,128)(2,1)} %wi_ref.1, ...), custom_call_target="tpu_custom_call" | custom-call | tf_op jit(solution)/shard_map/compute/pallas_call | solution.py:335
  11.2 43.5 %exchange.1 = bf16[2,2,8,4,16,128]{5,4,3,2,1,0:T(8,128)(2,1)} custom-call(bf16[2,2,8,4,16,128]{5,4,3,2,1,0:T(8,128)(2,1)} %bitcast.7), custom_call_target="tpu_custom_call" | custom-call | tf_op jit(solution)/shard_map/exchange/pallas_call | solution.py:366
  54.7 2.0 %finish.1 = (bf16[288,384]{1,0:T(8,128)(2,1)}, bf16[1,384]{1,0:T(2,128)(2,1)}, bf16[288,384]{1,0:T(8,128)(2,1)}, bf16[1,384]{1,0:T(2,128)(2,1)}, bf16[1,768]{1,0:T(2,128)(2,1)}, /*index=5*/bf16[1,768]{1,0:T(2,128)(2,1)}) custom-call(bf16[2,64,16,128]{3,2,1,0:T(8,128)(2,1)} %bitcast.6), custom_call_target="tpu_custom_call" | custom-call | tf_op jit(solution)/shard_map/finish/pallas_call | solution.py:389
  56.7 0.0 copy-start.7
  56.7 0.7 %copy-done.7 = bf16[1,384]{1,0:T(2,128)(2,1)S(1)} copy-done((bf16[1,384]{1,0:T(2,128)(2,1)S(1)}, bf16[1,384]{1,0:T(2,128)(2,1)}, u32[]{:S(2)}) %copy-start.7) | copy-done | bytes 792
  57.4 0.6 reduce
  58.0 0.0 copy-done.6
  58.0 0.6 slice_reduce_fusion
  58.5 0.0 copy-done.3
  58.6 0.6 reduce.2
  59.1 0.1 copy-done.2
  59.2 0.6 reduce.3
  (3 shorter events, 0.0 us)
Async XLA Ops:
  0.6 0.7 %copy-start.4 = (s32[320]{0:T(512)S(1)}, s32[320]{0:T(512)}, u32[]{:S(2)}) copy-start(s32[320]{0:T(512)} %param.12) | copy-start | bytes 3844
  0.6 1.2 %copy-start.5 = (f32[384]{0:T(512)S(1)}, f32[384]{0:T(512)}, u32[]{:S(2)}) copy-start(f32[384]{0:T(512)} %param.16) | copy-start | bytes 4612
  0.7 1.8 %copy-start = (f32[768]{0:T(1024)S(1)}, f32[768]{0:T(1024)}, u32[]{:S(2)}) copy-start(f32[768]{0:T(1024)} %param.18) | copy-start | bytes 9220
  2.4 0.7 %copy-start.1 = (f32[768]{0:T(1024)S(1)}, f32[768]{0:T(1024)}, u32[]{:S(2)}) copy-start(f32[768]{0:T(1024)} %param.19) | copy-start | bytes 9220
  56.7 0.7 %copy-start.7 = (bf16[1,384]{1,0:T(2,128)(2,1)S(1)}, bf16[1,384]{1,0:T(2,128)(2,1)}, u32[]{:S(2)}) copy-start(bf16[1,384]{1,0:T(2,128)(2,1)} %get-tuple-element.18) | copy-start | bytes 2308
  56.7 1.3 %copy-start.6 = (bf16[1,384]{1,0:T(2,128)(2,1)S(1)}, bf16[1,384]{1,0:T(2,128)(2,1)}, u32[]{:S(2)}) copy-start(bf16[1,384]{1,0:T(2,128)(2,1)} %get-tuple-element.20) | copy-start | bytes 2308
  57.4 1.2 %copy-start.3 = (bf16[1,768]{1,0:T(2,128)(2,1)S(1)}, bf16[1,768]{1,0:T(2,128)(2,1)}, u32[]{:S(2)}) copy-start(bf16[1,768]{1,0:T(2,128)(2,1)} %get-tuple-element.21) | copy-start | bytes 4612
  58.5 0.7 %copy-start.2 = (bf16[1,768]{1,0:T(2,128)(2,1)S(1)}, bf16[1,768]{1,0:T(2,128)(2,1)}, u32[]{:S(2)}) copy-start(bf16[1,768]{1,0:T(2,128)(2,1)} %get-tuple-element.22) | copy-start | bytes 4612

commit v2 on v1

--- a/solution.py
+++ b/solution.py
@@ -15,8 +15,8 @@
 H = 384
 NX = 4
 SPANS = (288, 160, 96)
-BASES = (0, 288, 448)
-PAD_ROWS = ROWS + PMAX
+BASES = (0, 9, 14)
+PAD_TILES = TILES + PMAX // TILE
 LINES = 16
 BLOCKS = 64
 ENTRIES = 2 * PMAX * H + H + PMAX + 2 * C
@@ -28,7 +28,7 @@
 MESH = pl.DeviceIdType.MESH
 AXES = ("dp", "group")
 VMEM = pl.BlockSpec(memory_space=pltpu.VMEM)
-SMEM = pl.BlockSpec(memory_space=pltpu.SMEM)
+HBM = pl.BlockSpec(memory_space=pltpu.HBM)
 
 
 def dot(a, b, da, db):
@@ -62,9 +62,16 @@
     return images
 
 
-def compute_kernel(
-    tiles_ref, patches_ref, tok_ref, cot_ref, mask_ref, wi_ref, bi_ref, wo_ref, gain_ref, shift_ref,
-    dtok_ref, pack_ref,
+def rows_of(images, t, dn_ref, alive_ref):
+    source = jnp.int32(0)
+    for j, (tiles, start, _) in enumerate(images):
+        held = (start <= t) & (t < start + tiles)
+        source = jnp.where(held, BASES[j] + t - start, source)
+    return dn_ref[source].astype(F32) * wide(alive_ref[t * TILE : (t + 1) * TILE, :])
+
+
+def gradients(
+    tiles_ref, patches_ref, tok_ref, cot_ref, mask_ref, wi_ref, bi_ref, wo_ref, gain_ref, shift_ref, pack_ref,
     nx_ref, inv_ref, alive_ref, x_ref, d_ref, dn_ref, act_ref, dpre_ref, gi_ref, go_ref, bo_ref, small_ref,
 ):
     place = lax.axis_index("dp") * lax.axis_size("group") + lax.axis_index("group")
@@ -74,11 +81,11 @@
     for _, start, count in images:
         first = start * TILE
         alive = jnp.where((row >= first) & (row < first + count), 1.0, alive)
-    alive_ref[...] = alive * column(mask_ref[...].astype(F32))
-    gain = gain_ref[...]
-    shift = shift_ref[...]
-    x_ref[ROWS:, :] = jnp.zeros((PMAX, C), BF16)
-    d_ref[ROWS:, :] = jnp.zeros((PMAX, C), BF16)
+    alive_ref[...] = alive * column(mask_ref[...].astype(F32).reshape(1, ROWS))
+    gain = gain_ref[...].reshape(1, C)
+    shift = shift_ref[...].reshape(1, C)
+    x_ref[TILES:] = jnp.zeros((PMAX // TILE, TILE, C), BF16)
+    d_ref[TILES:] = jnp.zeros((PMAX // TILE, TILE, C), BF16)
     for t in range(TILES):
         rows = slice(t * TILE, (t + 1) * TILE)
         live = wide(alive_ref[rows, :])
@@ -88,20 +95,20 @@
         normal = center * inv
         nx_ref[rows, :] = normal
         inv_ref[rows, :] = jnp.broadcast_to(inv, (TILE, 128))
-        x_ref[rows, :] = ((normal * gain + shift) * live).astype(BF16)
-        d_ref[rows, :] = (cot_ref[rows, :].astype(F32) * live).astype(BF16)
-
-    bias = column(bi_ref[...])
+        x_ref[t] = ((normal * gain + shift) * live).astype(BF16)
+        d_ref[t] = (cot_ref[rows, :].astype(F32) * live).astype(BF16)
+
+    bias = column(bi_ref[...].reshape(1, H))
     ones = jnp.ones((16, C), BF16)
     bo_ref[...] = jnp.zeros((16, H), F32)
     sums = [jnp.zeros((128, 128), F32) for _ in range(3)]
     for j, (tiles, start, _) in enumerate(images):
         span = SPANS[j]
-        first = pl.multiple_of(start * TILE, TILE)
+        steps = range(span // TILE)
         inside = lax.broadcasted_iota(jnp.int32, (span, 128), 0) < tiles * TILE
         inside = wide(inside.astype(F32).astype(BF16))
-        xs = x_ref[pl.ds(first, span), :] * inside
-        ds = d_ref[pl.ds(first, span), :] * inside
+        xs = jnp.concatenate([x_ref[start + u] for u in steps]) * inside
+        ds = jnp.concatenate([d_ref[start + u] for u in steps]) * inside
         for h in range(3):
             lines = slice(h * 128, (h + 1) * 128)
             preact = dot(wi_ref[:span, lines], xs, 0, 0) + wide(bias[lines, :])
@@ -123,27 +130,18 @@
             gi_ref[:span, :] += gi
             go_ref[:span, :] += go
             bo_ref[:, :span] += bo
-        dn_ref[BASES[j] : BASES[j] + span, :] = dot(wi_ref[:span, :], dpre_ref[...], 1, 0).astype(BF16)
+        back = dot(wi_ref[:span, :], dpre_ref[...], 1, 0).astype(BF16)
+        for u in steps:
+            dn_ref[BASES[j] + u] = back[u * TILE : (u + 1) * TILE]
 
     gain_sum = jnp.zeros((8, C), F32)
     shift_sum = jnp.zeros((8, C), F32)
     for t in range(TILES):
-        rows = slice(t * TILE, (t + 1) * TILE)
-        source = jnp.int32(0)
-        for j, (tiles, start, _) in enumerate(images):
-            held = (start <= t) & (t < start + tiles)
-            source = jnp.where(held, BASES[j] + (t - start) * TILE, source)
-        source = pl.multiple_of(source, TILE)
-        normal = nx_ref[rows, :]
-        d_rows = dn_ref[pl.ds(source, TILE), :].astype(F32) * wide(alive_ref[rows, :])
-        weighted = d_rows * normal
+        d_rows = rows_of(images, t, dn_ref, alive_ref)
+        weighted = d_rows * nx_ref[t * TILE : (t + 1) * TILE, :]
         for i in range(0, TILE, 8):
             gain_sum = gain_sum + weighted[i : i + 8]
             shift_sum = shift_sum + d_rows[i : i + 8]
-        scaled = d_rows * gain
-        inner = jnp.mean(scaled * normal, axis=1, keepdims=True)
-        d_norm = (scaled - jnp.mean(scaled, axis=1, keepdims=True) - normal * inner) * wide(inv_ref[rows, :])
-        dtok_ref[rows, :] = (cot_ref[rows, :].astype(F32) + d_norm).astype(BF16)
 
     small_ref[...] = jnp.zeros((2 * LINES, 128), F32)
     gain_row = jnp.sum(gain_sum, axis=0, keepdims=True)
@@ -154,15 +152,35 @@
     for b in range(3):
         small_ref[16 + b : 17 + b, :] = jnp.sum(jnp.transpose(sums[b]), axis=0, keepdims=True)
         small_ref[19 + b : 20 + b, :] = bo_ref[0:1, b * 128 : (b + 1) * 128]
+    n, nx, lines = pack_ref.shape[2:5]
+    each = lines // LINES
+
+    def put(k, i, value):
+        shard, at = i // each, i % each * LINES
+        pack_ref[k, shard // (n * nx), shard // nx % n, shard % nx, at : at + LINES] = value
+
     for i in range(PMAX // LINES):
         for b in range(3):
             box = (slice(i * LINES, (i + 1) * LINES), slice(b * 128, (b + 1) * 128))
-            pack_ref[0, i * 3 + b] = gi_ref[box].astype(BF16)
-            pack_ref[1, i * 3 + b] = go_ref[box].astype(BF16)
-    pack_ref[0, 54] = small_ref[:LINES, :].astype(BF16)
-    pack_ref[0, 55] = small_ref[LINES:, :].astype(BF16)
-    pack_ref[0, 56:] = jnp.zeros((8, LINES, 128), BF16)
-    pack_ref[1, 54:] = jnp.zeros((10, LINES, 128), BF16)
+            put(0, i * 3 + b, gi_ref[box].astype(BF16))
+            put(1, i * 3 + b, go_ref[box].astype(BF16))
+    put(0, 54, small_ref[:LINES, :].astype(BF16))
+    put(0, 55, small_ref[LINES:, :].astype(BF16))
+    for k, used in ((0, 56), (1, 54)):
+        for i in range(used, BLOCKS):
+            put(k, i, jnp.zeros((LINES, 128), BF16))
+    return images
+
+
+def token_gradient(images, cot_ref, gain_ref, dtok_ref, nx_ref, inv_ref, alive_ref, dn_ref):
+    gain = gain_ref[...].reshape(1, C)
+    for t in range(TILES):
+        rows = slice(t * TILE, (t + 1) * TILE)
+        normal = nx_ref[rows, :]
+        scaled = rows_of(images, t, dn_ref, alive_ref) * gain
+        inner = jnp.mean(scaled * normal, axis=1, keepdims=True)
+        d_norm = (scaled - jnp.mean(scaled, axis=1, keepdims=True) - normal * inner) * wide(inv_ref[rows, :])
+        dtok_ref[rows, :] = (cot_ref[rows, :].astype(F32) + d_norm).astype(BF16)
 
 
 def ring_order(n):
@@ -183,12 +201,22 @@
     return copy
 
 
-def comm_kernel(
+def main_kernel(
     nx, ny, nz,
-    pack_ref, out_ref,
-    r0, q, r1, t_ref, r2, u_ref, r3,
+    tiles_in, patches_in, tok_in, cot_in, mask_in, wi_in, bi_in, wo_in, gain_in, shift_in,
+    dtok_ref, out_ref,
+    tiles_ref, patches_ref, tok_ref, cot_ref, mask_ref, wi_ref, bi_ref, wo_ref, gain_ref, shift_ref, in_sem,
+    nx_ref, inv_ref, alive_ref, x_ref, d_ref, dn_ref, act_ref, dpre_ref, gi_ref, go_ref, bo_ref, small_ref,
+    pack_ref, r0, q, r1, t_ref, r2, u_ref, r3,
     s0, v0, s1, v1, s2, v2, s3, v3, s4, v4, s5, v5, s6, v6,
 ):
+    pairs = (
+        (tok_in, tok_ref), (mask_in, mask_ref), (gain_in, gain_ref), (shift_in, shift_ref), (tiles_in, tiles_ref),
+        (patches_in, patches_ref), (cot_in, cot_ref), (wi_in, wi_ref), (wo_in, wo_ref), (bi_in, bi_ref),
+    )
+    loads = [pltpu.make_async_copy(a, b, in_sem.at[i]) for i, (a, b) in enumerate(pairs)]
+    for load in loads:
+        load.start()
     dp = lax.axis_index("dp")
     group = lax.axis_index("group")
     y, x = dp // nx, lax.rem(dp, nx)
@@ -215,6 +243,12 @@
     everyone += [x_peer(d) for d in range(1, nx)]
     for device in everyone:
         pl.semaphore_signal(barrier, inc=1, device_id=device, device_id_type=MESH)
+    for load in loads:
+        load.wait()
+    images = gradients(
+        tiles_ref, patches_ref, tok_ref, cot_ref, mask_ref, wi_ref, bi_ref, wo_ref, gain_ref, shift_ref, pack_ref,
+        nx_ref, inv_ref, alive_ref, x_ref, d_ref, dn_ref, act_ref, dpre_ref, gi_ref, go_ref, bo_ref, small_ref,
+    )
     pl.semaphore_wait(barrier, len(everyone))
     copies = []
 
@@ -242,6 +276,7 @@
                         q.at[k, at], r1.at[k, mine[k]], (s1.at[k, d], v1.at[k, d]), peers[k](d)
                     )
                     copies.append(second[k, d])
+    token_gradient(images, cot_ref, gain_ref, dtok_ref, nx_ref, inv_ref, alive_ref, dn_ref)
     for k in (0, 1):
         total = q[k, mine[k]].astype(F32)
         for d in ring_order(chip[k]):
@@ -305,7 +340,8 @@
         copy.wait_send()
 
 
-def finish_kernel(sum_ref, wi_ref, bi_ref, wo_ref, bo_ref, gain_ref, shift_ref):
+def finish_kernel(dtok_ref, sum_ref, out_ref, wi_ref, bi_ref, wo_ref, bo_ref, gain_ref, shift_ref):
+    out_ref[...] = dtok_ref[...]
     total = jnp.zeros((LINES, 128), F32)
     for k in (0, 1):
         for i in range(56 - 2 * k):
@@ -321,55 +357,53 @@
     one = sum_ref[0, 54].astype(F32) * factor
     two = sum_ref[0, 55].astype(F32) * factor
     for b in range(6):
-        at = slice(b * 128, (b + 1) * 128)
-        gain_ref[:, at] = one[b : b + 1].astype(BF16)
-        shift_ref[:, at] = one[6 + b : 7 + b].astype(BF16)
+        at = pl.ds(b * 128, 128)
+        gain_ref[at] = one[b].astype(BF16)
+        shift_ref[at] = one[6 + b].astype(BF16)
     for b in range(3):
-        at = slice(b * 128, (b + 1) * 128)
-        bi_ref[:, at] = two[b : b + 1].astype(BF16)
-        bo_ref[:, at] = two[3 + b : 4 + b].astype(BF16)
-
-
-def compute(tokens, cotangent, patch_mask, image_tiles, patches, w_in, b_in, w_out, ln_gain, ln_shift):
-    shape = jax.ShapeDtypeStruct
+        width = min(128, PMAX - b * 128)
+        bi_ref[pl.ds(b * 128, 128)] = two[b].astype(BF16)
+        bo_ref[pl.ds(b * 128, width)] = two[3 + b, :width].astype(BF16)
+
+
+def main(nx, ny, nz, tokens, cotangent, patch_mask, image_tiles, patches, *weights):
+    w_in, b_in, w_out, ln_gain, ln_shift = weights
+    args = (image_tiles.T, patches.T, tokens, cotangent, patch_mask, w_in, b_in, w_out.T, ln_gain, ln_shift)
+    n, places = max(ny, nz), image_tiles.shape[0]
+    shape, dma = jax.ShapeDtypeStruct, pltpu.SemaphoreType.DMA
+    block = (BLOCKS // (2 * n * nx) * LINES, 128)
+    sems = [(2, n), (2, n), (nx,), (2, n), (2, nx), (2, n), (2, n)]
     return pl.pallas_call(
-        compute_kernel,
-        name="compute",
-        out_shape=(shape((ROWS, C), BF16), shape((2, BLOCKS, LINES, 128), BF16)),
-        in_specs=[SMEM, SMEM] + [VMEM] * 8,
+        lambda *refs: main_kernel(nx, ny, nz, *refs),
+        name="main",
+        out_shape=(shape((ROWS, C), BF16), shape((2, 2, n, nx, *block), BF16)),
+        in_specs=[HBM] * 10,
         out_specs=(VMEM, VMEM),
         scratch_shapes=[
+            pltpu.SMEM((3, places), jnp.int32),
+            pltpu.SMEM((3, places), jnp.int32),
+            pltpu.VMEM((ROWS, C), BF16),
+            pltpu.VMEM((ROWS, C), BF16),
+            pltpu.VMEM((ROWS,), jnp.int32),
+            pltpu.VMEM((PMAX, H), BF16),
+            pltpu.VMEM((H,), F32),
+            pltpu.VMEM((PMAX, H), BF16),
+            pltpu.VMEM((C,), F32),
+            pltpu.VMEM((C,), F32),
+            dma((10,)),
             pltpu.VMEM((ROWS, C), F32),
             pltpu.VMEM((ROWS, 128), F32),
             pltpu.VMEM((ROWS, 128), F32),
-            pltpu.VMEM((PAD_ROWS, C), BF16),
-            pltpu.VMEM((PAD_ROWS, C), BF16),
-            pltpu.VMEM((sum(SPANS), C), BF16),
+            pltpu.VMEM((PAD_TILES, TILE, C), BF16),
+            pltpu.VMEM((PAD_TILES, TILE, C), BF16),
+            pltpu.VMEM((sum(SPANS) // TILE, TILE, C), BF16),
             pltpu.VMEM((H, C), BF16),
             pltpu.VMEM((H, C), BF16),
             pltpu.VMEM((PMAX, H), F32),
             pltpu.VMEM((PMAX, H), F32),
             pltpu.VMEM((16, H), F32),
             pltpu.VMEM((2 * LINES, 128), F32),
-        ],
-    )(
-        image_tiles.T, patches.T, tokens, cotangent, patch_mask.reshape(1, ROWS), w_in,
-        b_in.reshape(1, H), w_out.T, ln_gain.reshape(1, C), ln_shift.reshape(1, C),
-    )
-
-
-def total_of(packed, nx, ny, nz):
-    n = max(ny, nz)
-    dma = pltpu.SemaphoreType.DMA
-    block = (LINES, 128)
-    sems = [(2, n), (2, n), (nx,), (2, n), (2, nx), (2, n), (2, n)]
-    return pl.pallas_call(
-        lambda *refs: comm_kernel(nx, ny, nz, *refs),
-        name="exchange",
-        out_shape=jax.ShapeDtypeStruct((2, 2, n, nx, *block), BF16),
-        in_specs=[VMEM],
-        out_specs=VMEM,
-        scratch_shapes=[
+            pltpu.VMEM((2, 2, n, nx, *block), BF16),
             pltpu.VMEM((2, n, nx, *block), BF16),
             pltpu.VMEM((2, n, nx, *block), BF16),
             pltpu.VMEM((2, n, nx, *block), BF16),
@@ -379,32 +413,30 @@
             pltpu.VMEM((2, n, *block), BF16),
         ]
         + [dma(shape) for shape in sems for _ in range(2)],
-        compiler_params=pltpu.CompilerParams(collective_id=0, has_side_effects=True),
-    )(packed.reshape(2, 2, n, nx, *block))
-
-
-def finish(sums):
+        compiler_params=pltpu.CompilerParams(collective_id=0, has_side_effects=True, vmem_limit_bytes=20 << 20),
+    )(*[pltpu.with_memory_space_constraint(v, pltpu.HBM) for v in args])
+
+
+def finish(dtokens, sums):
     shape = jax.ShapeDtypeStruct
-    shapes = ((PMAX, H), (1, H), (PMAX, H), (1, H), (1, C), (1, C))
+    shapes = ((ROWS, C), (PMAX, H), (H,), (PMAX, H), (PMAX,), (C,), (C,))
     return pl.pallas_call(
         finish_kernel,
         name="finish",
         out_shape=tuple(shape(s, BF16) for s in shapes),
-        in_specs=[VMEM],
-        out_specs=(VMEM,) * 6,
-    )(sums)
+        in_specs=[VMEM, VMEM],
+        out_specs=(VMEM,) * 7,
+        compiler_params=pltpu.CompilerParams(vmem_limit_bytes=10 << 20),
+    )(dtokens, sums)
 
 
 def solution(mesh):
     ny, nz = mesh.shape["dp"] // NX, mesh.shape["group"] // 2
 
     def local(*args):
-        dtokens, packed = compute(*args)
-        sums = total_of(packed, NX, ny, nz).reshape(2, BLOCKS, LINES, 128)
-        w_in, b_in, w_out, b_out, gain, shift = finish(sums)
-        return (
-            dtokens, w_in, b_in.reshape(H), w_out.T, b_out.reshape(H)[:PMAX], gain.reshape(C), shift.reshape(C)
-        )
+        dtokens, sums = main(NX, ny, nz, *args)
+        dtokens, w_in, b_in, w_out, b_out, gain, shift = finish(dtokens, sums.reshape(2, BLOCKS, LINES, 128))
+        return (dtokens, w_in, b_in, w_out.T, b_out, gain, shift)
 
     rows = P(AXES, None)
     in_specs = (rows, rows, P(AXES)) + (P(),) * 7

time: 60.2 us -> 45.7 us (0.76)
  Pallas kernels: 53 us -> 44.9 us
  local copies, waits for them, and re-layouts: 4.4 us -> 0 us
  other arithmetic: 1.77 us -> 0 us
    pallas_call x2 -> x1, Pallas kernels: 51 us -> 43.7 us  [main(): pl.pallas_call(lambda *refs: main_kernel(nx, ny, nz, *refs), name='main',...]
    reshape x4 -> x0, local copies, waits for them, and re-layouts: 2.29 us -> none  [the longest x1 0.58 us: compute(): ln_gain.reshape(1, C)]
    pallas_call x3 -> x0, other arithmetic: 1.77 us -> none  [finish(): pl.pallas_call(finish_kernel, name='finish', out_shape=tuple((shape(s, BF...]
    unnamed x16 -> x0, local copies, waits for them, and re-layouts: 1.53 us -> none
    pallas_call x1, Pallas kernels: 2.02 us -> 1.14 us  [finish(): pl.pallas_call(finish_kernel, name='finish', out_shape=tuple((shape(s, BF...]
where the time goes in v2:
time: 45.7 us; the launch traced here: 45.5 us
  Pallas kernels  44.9 us (98%)
  between operations  0.64 us (1%)
    pallas_call x1, Pallas kernels, main(): pl.pallas_call(lambda *refs: main_kernel(nx, ny, nz, *refs), name='main',...  43.7 us
    pallas_call x1, Pallas kernels, finish(): pl.pallas_call(finish_kernel, name='finish', out_shape=tuple((shape(s, BF...  1.14 us

profile of v2, /device:TPU:1, one launch (start us, length us, event | category | flops | bytes accessed | tf_op | source)
XLA Modules:
  0.0 45.5 jit_solution(5212744545326735381)
XLA Ops:
  0.6 43.7 %main.1 = (bf16[320,768]{1,0:T(8,128)(2,1)S(1)}, bf16[2,2,8,4,16,128]{5,4,3,2,1,0:T(8,128)(2,1)S(1)}) custom-call(s32[3,512]{1,0:T(4,128)} %bitcast.7, s32[3,512]{1,0:T(4,128)} %bitcast.8, bf16[320,768]{1,0:T(8,128)(2,1)} %refs_2_.1, bf16[320,768]{1,0:T(8,128)(2,1)} %refs_3_.1, s32[320]{0:T(512)} %refs_4_.1, bf16[288,384]{1,0:T(8,128)(2,1)} %refs_5_.1, ...), custom_call_target="tpu_custom_call" | custom-call | tf_op jit(solution)/shard_map/main/pallas_call | solution.py:376
  44.4 1.1 %finish.1 = (bf16[320,768]{1,0:T(8,128)(2,1)}, bf16[288,384]{1,0:T(8,128)(2,1)}, bf16[384]{0:T(512)(128)(2,1)}, bf16[288,384]{1,0:T(8,128)(2,1)}, bf16[288]{0:T(...) custom-call(bf16[320,768]{1,0:T(8,128)(2,1)S(1)} %get-tuple-element.16.dtok_ref, ...), custom_call_target="tpu_custom_call" | custom-call | tf_op jit(solution)/shard_map/finish/pallas_call | solution.py:423

commit v3 on v2

v3 whole, which is shorter than its diff:
```python
import math

import jax
import jax.numpy as jnp
from jax import lax
from jax.experimental import pallas as pl
from jax.experimental.pallas import tpu as pltpu
from jax.sharding import PartitionSpec as P

PMAX = 288
TILE = 32
TILES = 10
ROWS = TILE * TILES
C = 768
H = 384
NX = 4
SPANS = (288, 160, 96)
BASES = (0, 9, 14)
PAD_TILES = TILES + PMAX // TILE
LINES = 16
BLOCKS = 64
ENTRIES = 2 * PMAX * H + H + PMAX + 2 * C

ln_epsilon = 1e-05
clip_share = 0.5
F32 = jnp.float32
BF16 = jnp.bfloat16
MESH = pl.DeviceIdType.MESH
AXES = ("dp", "group")
VMEM = pl.BlockSpec(memory_space=pltpu.VMEM)
HBM = pl.BlockSpec(memory_space=pltpu.HBM)


def dot(a, b, da, db):
    return lax.dot_general(a, b, (((da,), (db,)), ((), ())), preferred_element_type=F32)


def gelu_pair(preact):
    scaled = preact * 0.7071067811865476
    normal_cdf = 0.5 * lax.erf(scaled) + 0.5
    density = jnp.exp2(scaled * scaled * -1.4426950408889634)
    return (preact * normal_cdf, normal_cdf + preact * 0.3989422804014327 * density)


def wide(col):
    return jnp.concatenate([col] * (C // 128), axis=1)


def column(row):
    return jnp.transpose(jnp.broadcast_to(row, (128, row.shape[1])))


def image_table(tiles_ref, patches_ref, place):
    tiles = [tiles_ref[s, place] for s in range(3)]
    counts = [patches_ref[s, place] for s in range(3)]
    starts = [jnp.int32(0), tiles[0], tiles[0] + tiles[1]]
    images = list(zip(tiles, starts, counts))
    for i, j in ((0, 1), (0, 2), (1, 2)):
        a, b = images[i], images[j]
        swap = b[0] > a[0]
        images[i] = tuple(jnp.where(swap, q, p) for p, q in zip(a, b))
        images[j] = tuple(jnp.where(swap, p, q) for p, q in zip(a, b))
    return images


def rows_of(images, t, dn_ref, alive_ref):
    source = jnp.int32(0)
    for j, (tiles, start, _) in enumerate(images):
        held = (start <= t) & (t < start + tiles)
        source = jnp.where(held, BASES[j] + t - start, source)
    return dn_ref[source].astype(F32) * wide(alive_ref[t * TILE : (t + 1) * TILE, :])


def gradients(
    loads, tiles_ref, patches_ref, tok_ref, cot_ref, mask_ref, wi_ref, bi_ref, wo_ref, gain_ref, shift_ref, pack_ref,
    nx_ref, inv_ref, alive_ref, x_ref, d_ref, dn_ref, act_ref, dpre_ref, gi_ref, go_ref, bo_ref, small_ref,
    xs_ref, ds_ref, pre_ref, dz_ref, sum_ref, wt_ref, ro_ref, late_ref,
):
    place = lax.axis_index("dp") * lax.axis_size("group") + lax.axis_index("group")
    x_ref[TILES:] = jnp.zeros((PMAX // TILE, TILE, C), BF16)
    d_ref[TILES:] = jnp.zeros((PMAX // TILE, TILE, C), BF16)
    sum_ref[...] = jnp.zeros((H, 128), F32)
    ro_ref[TILES:] = jnp.zeros((PMAX // TILE, TILE, 128), F32)
    small_ref[...] = jnp.zeros((LINES, 128), F32)
    late_ref[...] = jnp.zeros((LINES, 128), F32)
    for load in loads[:6]:
        load.wait()
    images = image_table(tiles_ref, patches_ref, place)
    row = lax.broadcasted_iota(jnp.int32, (ROWS, 128), 0)
    alive = jnp.zeros((ROWS, 128), F32)
    for _, start, count in images:
        first = start * TILE
        alive = jnp.where((row >= first) & (row < first + count), 1.0, alive)
    alive_ref[...] = alive * column(mask_ref[...].astype(F32).reshape(1, ROWS))
    gain = gain_ref[...].reshape(1, C)
    shift = shift_ref[...].reshape(1, C)
    for t in range(TILES):
        rows = slice(t * TILE, (t + 1) * TILE)
        values = tok_ref[rows, :].astype(F32)
        center = values - jnp.mean(values, axis=1, keepdims=True)
        inv = lax.rsqrt(jnp.mean(center * center, axis=1, keepdims=True) + ln_epsilon)
        normal = center * inv
        nx_ref[rows, :] = normal
        inv_ref[rows, :] = jnp.broadcast_to(inv, (TILE, 128))
        x_ref[t] = ((normal * gain + shift) * wide(alive_ref[rows, :])).astype(BF16)
    for load in loads[6:]:
        load.wait()
    for t in range(TILES):
        rows = slice(t * TILE, (t + 1) * TILE)
        dout = (cot_ref[rows, :].astype(F32) * wide(alive_ref[rows, :])).astype(BF16)
        d_ref[t] = dout
        ro_ref[t] = jnp.broadcast_to(jnp.sum(dout.astype(F32), axis=1, keepdims=True), (TILE, 128))

    bias = column(bi_ref[...].reshape(1, H))
    bias = jnp.concatenate([bias, bias], axis=1)
    wt_ref[0] = jnp.transpose(wi_ref[...])
    wt_ref[1] = jnp.transpose(wo_ref[...])
    bo_ref[...] = jnp.zeros((H, 128), F32)

    def place_rows(j):
        tiles, start, _ = images[j]
        for u in range(SPANS[j] // TILE):
            held = jnp.where(u < tiles, 1.0, 0.0)
            keep = held.astype(BF16)
            bo_ref[u * TILE : (u + 1) * TILE, :] += ro_ref[start + u] * held
            at = slice((BASES[j] + u) * TILE, (BASES[j] + u + 1) * TILE)
            xs_ref[at, :] = x_ref[start + u] * keep
            ds_ref[at, :] = d_ref[start + u] * keep

    def own(j):
        return slice(BASES[j] * TILE, BASES[j] * TILE + SPANS[j])

    def project(j, part):
        cols = slice(part * 256, (part + 1) * 256)
        pre_ref[j % 2, :, cols] = dot(wt_ref[0, :, : SPANS[j]], xs_ref[own(j), cols], 1, 0)
        dz_ref[j % 2, :, cols] = dot(wt_ref[1, :, : SPANS[j]], ds_ref[own(j), cols], 1, 0)

    def activate(j, part):
        cols = slice(part * 256, (part + 1) * 256)
        act, slope = gelu_pair(pre_ref[j % 2, :, cols] + bias)
        act_ref[j, :, cols] = act.astype(BF16)
        dpre = dz_ref[j % 2, :, cols] * slope
        dpre_ref[j, :, cols] = dpre.astype(BF16)
        sum_ref[...] += dpre[:, :128] + dpre[:, 128:]

    def reduce(j, part):
        span = SPANS[j]
        if part == 0:
            gi = dot(xs_ref[own(j), :], dpre_ref[j], 1, 1)
            gi_ref[:span, :] = gi if j == 0 else gi_ref[:span, :] + gi
        elif part == 1:
            go = dot(ds_ref[own(j), :], act_ref[j], 1, 1)
            go_ref[:span, :] = go if j == 0 else go_ref[:span, :] + go

    for j in range(3):
        place_rows(j)
    for step in range(5):
        for part in range(3):
            if step < 3:
                project(step, part)
            if 1 <= step < 4:
                activate(step - 1, part)
            if step >= 2:
                reduce(step - 2, part)

    for b in range(3):
        small_ref[b : b + 1, :] = jnp.sum(jnp.transpose(sum_ref[b * 128 : (b + 1) * 128, :]), axis=0, keepdims=True)
        small_ref[3 + b : 4 + b, :] = jnp.transpose(bo_ref[b * 128 : (b + 1) * 128, :])[0:1]
    n, nx, lines = pack_ref.shape[2:5]
    each = lines // LINES

    def put(k, i, value):
        shard, at = i // each, i % each * LINES
        pack_ref[k, shard // (n * nx), shard // nx % n, shard % nx, at : at + LINES] = value

    for i in range(PMAX // LINES):
        for b in range(3):
            box = (slice(i * LINES, (i + 1) * LINES), slice(b * 128, (b + 1) * 128))
            put(0, i * 3 + b, gi_ref[box].astype(BF16))
            put(1, i * 3 + b, go_ref[box].astype(BF16))
    put(0, 54, small_ref[...].astype(BF16))
    for k, used in ((0, 55), (1, 54)):
        for i in range(used, BLOCKS):
            put(k, i, jnp.zeros((LINES, 128), BF16))
    return images


def late_sums(images, wi_ref, dpre_ref, dn_ref, nx_ref, alive_ref, late_ref, bl_ref):
    for j in range(3):
        back_rows = dot(wi_ref[: SPANS[j], :], dpre_ref[j], 1, 0).astype(BF16)
        for u in range(SPANS[j] // TILE):
            dn_ref[BASES[j] + u] = back_rows[u * TILE : (u + 1) * TILE]
    gain_sum = jnp.zeros((8, C), F32)
    shift_sum = jnp.zeros((8, C), F32)
    for t in range(TILES):
        d_rows = rows_of(images, t, dn_ref, alive_ref)
        weighted = d_rows * nx_ref[t * TILE : (t + 1) * TILE, :]
        for i in range(0, TILE, 8):
            gain_sum = gain_sum + weighted[i : i + 8]
            shift_sum = shift_sum + d_rows[i : i + 8]

    gain_row = jnp.sum(gain_sum, axis=0, keepdims=True)
    shift_row = jnp.sum(shift_sum, axis=0, keepdims=True)
    for b in range(6):
        late_ref[b : b + 1, :] = gain_row[:, b * 128 : (b + 1) * 128]
        late_ref[6 + b : 7 + b, :] = shift_row[:, b * 128 : (b + 1) * 128]
    bl_ref[...] = late_ref[...].astype(BF16)


def token_gradient(images, cot_ref, gain_ref, dtok_ref, nx_ref, inv_ref, alive_ref, dn_ref):
    gain = gain_ref[...].reshape(1, C)
    for t in range(TILES):
        rows = slice(t * TILE, (t + 1) * TILE)
        normal = nx_ref[rows, :]
        scaled = rows_of(images, t, dn_ref, alive_ref) * gain
        inner = jnp.mean(scaled * normal, axis=1, keepdims=True)
        d_norm = (scaled - jnp.mean(scaled, axis=1, keepdims=True) - normal * inner) * wide(inv_ref[rows, :])
        dtok_ref[rows, :] = (cot_ref[rows, :].astype(F32) + d_norm).astype(BF16)


def ring_order(n):
    order = []
    for d in range(1, n // 2 + 1):
        order.append(d)
        if n - d != d:
            order.append(n - d)
    return order


def main_kernel(
    nx, ny, nz,
    tiles_in, patches_in, tok_in, cot_in, mask_in, wi_in, bi_in, wo_in, gain_in, shift_in,
    dtok_ref, out_ref, late_out,
    tiles_ref, patches_ref, tok_ref, cot_ref, mask_ref, wi_ref, bi_ref, wo_ref, gain_ref, shift_ref, in_sem,
    nx_ref, inv_ref, alive_ref, x_ref, d_ref, dn_ref, act_ref, dpre_ref, gi_ref, go_ref, bo_ref, small_ref,
    xs_ref, ds_ref, pre_ref, dz_ref, sum_ref, wt_ref, ro_ref, late_ref,
    bl_ref, lc, lz, lx, ly, sl, vl,
    pack_ref, r0, q, r1, t_ref, r2, u_ref, r3,
    s0, v0, s1, v1, s2, v2, s3, v3, s4, v4, s5, v5, s6, v6,
):
    pairs = (
        (tok_in, tok_ref), (mask_in, mask_ref), (gain_in, gain_ref), (shift_in, shift_ref), (tiles_in, tiles_ref),
        (patches_in, patches_ref), (cot_in, cot_ref), (wi_in, wi_ref), (wo_in, wo_ref), (bi_in, bi_ref),
    )
    loads = [pltpu.make_async_copy(a, b, in_sem.at[i]) for i, (a, b) in enumerate(pairs)]
    for load in loads:
        load.start()
    dp = lax.axis_index("dp")
    group = lax.axis_index("group")
    y, x = dp // nx, lax.rem(dp, nx)
    z, c = group // 2, lax.rem(group, 2)
    mate = 1 - c
    chip = (nz, ny)
    mine = (z, y)
    partner = (dp, z * 2 + mate)

    def z_peer(d):
        return (dp, lax.rem(z + d, nz) * 2 + c)

    def y_peer(d):
        return (lax.rem(y + d, ny) * nx + x, group)

    def x_peer(d):
        return (y * nx + lax.rem(x + d, nx), group)

    peers = (z_peer, y_peer)
    barrier = pltpu.get_barrier_semaphore()
    everyone = [partner]
    everyone += [z_peer(d) for d in range(1, nz)]
    everyone += [y_peer(d) for d in range(1, ny)]
    everyone += [x_peer(d) for d in range(1, nx)]
    for device in everyone:
        pl.semaphore_signal(barrier, inc=1, device_id=device, device_id_type=MESH)
    images = gradients(
        loads, tiles_ref, patches_ref, tok_ref, cot_ref, mask_ref, wi_ref, bi_ref, wo_ref, gain_ref, shift_ref, pack_ref,
        nx_ref, inv_ref, alive_ref, x_ref, d_ref, dn_ref, act_ref, dpre_ref, gi_ref, go_ref, bo_ref, small_ref,
        xs_ref, ds_ref, pre_ref, dz_ref, sum_ref, wt_ref, ro_ref, late_ref,
    )
    pl.semaphore_wait(barrier, len(everyone))
    def send(source, target, send_sem, recv_sem, device):
        copy = pltpu.make_async_remote_copy(
            src_ref=source, dst_ref=target, send_sem=send_sem, recv_sem=recv_sem, device_id=device, device_id_type=MESH
        )
        copy.start()
        return copy

    def drain(ref, sem):
        pltpu.make_async_copy(ref, ref, sem).wait()

    def back(at, d, n):
        return lax.rem(at - d + n, n)

    places = ((lc, 2, c, lambda d: partner), (lz, nz, z, z_peer), (lx, nx, x, x_peer), (ly, ny, y, y_peer))

    def late_send(stage):
        slots, n, at, peer = places[stage]
        for d in reversed(ring_order(n)):
            send(bl_ref.at[stage], slots.at[at], sl.at[stage], vl.at[stage], peer(d))
        slots[at] = bl_ref[stage]

    def late_wait(stage):
        slots, n, _, _ = places[stage]
        drain(slots.at[pl.ds(0, n - 1)], vl.at[stage])
        total = slots[0].astype(F32)
        for i in range(1, n):
            total = total + slots[i].astype(F32)
        return total.astype(BF16)

    near = ring_order(nx)
    rings = [ring_order(m) for m in chip]
    rest = [pl.ds(0, m - 1) for m in chip]
    orders = [ring[::-1] + [0] for ring in rings]
    steps = [(k, orders[k][i]) for i in range(max(chip)) for k in (0, 1) if i < chip[k]]
    first = {}
    for k, d in steps:
        at = lax.rem(mine[k] + d, chip[k])
        first[k, d] = send(pack_ref.at[k, mate, at], r0.at[k, at], s0.at[k], v0.at[k, d], partner)
    for k, d in steps:
        at = lax.rem(mine[k] + d, chip[k])
        first[k, d].wait_recv()
        q[k, at] = (pack_ref[k, c, at].astype(F32) + r0[k, at].astype(F32)).astype(BF16)
        if d:
            send(q.at[k, at], r1.at[k, mine[k]], s1.at[k], v1.at[k], peers[k](d))
    late_sums(images, wi_ref, dpre_ref, dn_ref, nx_ref, alive_ref, late_ref, bl_ref.at[0])
    late_send(0)
    token_gradient(images, cot_ref, gain_ref, dtok_ref, nx_ref, inv_ref, alive_ref, dn_ref)
    for k in (0, 1):
        drain(r1.at[k, rest[k]], v1.at[k])
        total = q[k, mine[k]].astype(F32)
        for d in rings[k]:
            total = total + r1[k, back(mine[k], d, chip[k])].astype(F32)
        t_ref[:, k] = total.astype(BF16)
    for d in near[::-1]:
        send(t_ref.at[lax.rem(x + d, nx)], r2.at[x], s2.at[0], v2.at[0], x_peer(d))
    bl_ref[1] = late_wait(0)
    late_send(1)
    drain(r2.at[pl.ds(0, nx - 1)], v2.at[0])
    total = t_ref[x].astype(F32)
    for d in near:
        total = total + r2[back(x, d, nx)].astype(F32)
    u_ref[...] = total.astype(BF16)
    for k in (0, 1):
        for d in rings[1 - k][::-1]:
            send(u_ref.at[k], r3.at[k, mine[1 - k]], s3.at[k], v3.at[k], peers[1 - k](d))
        r3[k, mine[1 - k]] = u_ref[k]
    bl_ref[2] = late_wait(1)
    late_send(2)
    for k in (0, 1):
        drain(r3.at[k, rest[1 - k]], v3.at[k])
        total = r3[k, 0].astype(F32)
        for i in range(1, chip[1 - k]):
            total = total + r3[k, i].astype(F32)
        out_ref[k, c, mine[k], x] = total.astype(BF16)
        block = out_ref.at[k, c, mine[k], x]
        for d in near[::-1]:
            send(block, block, s4.at[k], v4.at[k], x_peer(d))
    bl_ref[3] = late_wait(2)
    late_send(3)
    sixth = {}
    for k in (0, 1):
        drain(out_ref.at[k, c, mine[k], pl.ds(0, nx - 1)], v4.at[k])
        block = out_ref.at[k, c, mine[k]]
        for d in rings[k]:
            sixth[k, d] = send(block, block, s5.at[k], v5.at[k, d], peers[k](d))
        send(block, block, s6.at[k], v6.at[k], partner)
    for i in range(max(chip) - 1):
        for k in (0, 1):
            if i < chip[k] - 1:
                d = rings[k][i]
                sixth[k, d].wait_recv()
                block = out_ref.at[k, c, back(mine[k], d, chip[k])]
                send(block, block, s6.at[k], v6.at[k], partner)
    late_out[...] = late_wait(3)
    for k in (0, 1):
        drain(out_ref.at[k, mate], v6.at[k])
        drain(pack_ref.at[k, mate], s0.at[k])
        drain(q.at[k, rest[k]], s1.at[k])
        drain(r3.at[k, rest[1 - k]], s3.at[k])
        drain(out_ref.at[k, c, mine[k], pl.ds(0, nx - 1)], s4.at[k])
        drain(q.at[k, rest[k]], s5.at[k])
        drain(out_ref.at[k, c], s6.at[k])
    drain(r2.at[pl.ds(0, nx - 1)], s2.at[0])
    for stage, (slots, n, _, _) in enumerate(places):
        drain(slots.at[pl.ds(0, n - 1)], sl.at[stage])


def finish_kernel(dtok_ref, sum_ref, late_ref, out_ref, wi_ref, bi_ref, wo_ref, bo_ref, gain_ref, shift_ref, sem):
    move = pltpu.make_async_copy(dtok_ref, out_ref, sem)
    move.start()
    one = late_ref[...].astype(F32)
    total = one * one
    for k in (0, 1):
        for i in range(55 - k):
            piece = sum_ref[k, i].astype(F32)
            total = total + piece * piece
    total = jnp.sum(jnp.sum(total, axis=1, keepdims=True), axis=0, keepdims=True)
    factor = jnp.minimum(1.0, clip_share * math.sqrt(ENTRIES) / jnp.sqrt(total + 1e-06))
    for i in range(PMAX // LINES):
        for b in range(3):
            box = (slice(i * LINES, (i + 1) * LINES), slice(b * 128, (b + 1) * 128))
            wi_ref[box] = (sum_ref[0, i * 3 + b].astype(F32) * factor).astype(BF16)
            wo_ref[box] = (sum_ref[1, i * 3 + b].astype(F32) * factor).astype(BF16)
    one = one * factor
    two = sum_ref[0, 54].astype(F32) * factor
    for b in range(6):
        at = pl.ds(b * 128, 128)
        gain_ref[at] = one[b].astype(BF16)
        shift_ref[at] = one[6 + b].astype(BF16)
    for b in range(3):
        width = min(128, PMAX - b * 128)
        bi_ref[pl.ds(b * 128, 128)] = two[b].astype(BF16)
        bo_ref[pl.ds(b * 128, width)] = two[3 + b, :width].astype(BF16)
    move.wait()


def main(nx, ny, nz, tokens, cotangent, patch_mask, image_tiles, patches, *weights):
    w_in, b_in, w_out, ln_gain, ln_shift = weights
    args = (image_tiles.T, patches.T, tokens, cotangent, patch_mask, w_in, b_in, w_out.T, ln_gain, ln_shift)
    n, places = max(ny, nz), image_tiles.shape[0]
    shape, dma = jax.ShapeDtypeStruct, pltpu.SemaphoreType.DMA
    block = (BLOCKS // (2 * n * nx) * LINES, 128)
    sems = [(2,), (2, n), (2,), (2,), (1,), (1,), (2,), (2,), (2,), (2,), (2,), (2, n), (2,), (2,)]
    return pl.pallas_call(
        lambda *refs: main_kernel(nx, ny, nz, *refs),
        name="main",
        out_shape=(shape((ROWS, C), BF16), shape((2, 2, n, nx, *block), BF16), shape((LINES, 128), BF16)),
        in_specs=[HBM] * 10,
        out_specs=(VMEM, VMEM, VMEM),
        scratch_shapes=[
            pltpu.SMEM((3, places), jnp.int32),
            pltpu.SMEM((3, places), jnp.int32),
            pltpu.VMEM((ROWS, C), BF16),
            pltpu.VMEM((ROWS, C), BF16),
            pltpu.VMEM((ROWS,), jnp.int32),
            pltpu.VMEM((PMAX, H), BF16),
            pltpu.VMEM((H,), F32),
            pltpu.VMEM((PMAX, H), BF16),
            pltpu.VMEM((C,), F32),
            pltpu.VMEM((C,), F32),
            dma((10,)),
            pltpu.VMEM((ROWS, C), F32),
            pltpu.VMEM((ROWS, 128), F32),
            pltpu.VMEM((ROWS, 128), F32),
            pltpu.VMEM((PAD_TILES, TILE, C), BF16),
            pltpu.VMEM((PAD_TILES, TILE, C), BF16),
            pltpu.VMEM((sum(SPANS) // TILE, TILE, C), BF16),
            pltpu.VMEM((3, H, C), BF16),
            pltpu.VMEM((3, H, C), BF16),
            pltpu.VMEM((PMAX, H), F32),
            pltpu.VMEM((PMAX, H), F32),
            pltpu.VMEM((H, 128), F32),
            pltpu.VMEM((LINES, 128), F32),
            pltpu.VMEM((sum(SPANS), C), BF16),
            pltpu.VMEM((sum(SPANS), C), BF16),
            pltpu.VMEM((2, H, C), F32),
            pltpu.VMEM((2, H, C), F32),
            pltpu.VMEM((H, 128), F32),
            pltpu.VMEM((2, H, PMAX), BF16),
            pltpu.VMEM((PAD_TILES, TILE, 128), F32),
            pltpu.VMEM((LINES, 128), F32),
            pltpu.VMEM((4, LINES, 128), BF16),
            pltpu.VMEM((2, LINES, 128), BF16),
            pltpu.VMEM((nz, LINES, 128), BF16),
            pltpu.VMEM((nx, LINES, 128), BF16),
            pltpu.VMEM((ny, LINES, 128), BF16),
            dma((4,)),
            dma((4,)),
            pltpu.VMEM((2, 2, n, nx, *block), BF16),
            pltpu.VMEM((2, n, nx, *block), BF16),
            pltpu.VMEM((2, n, nx, *block), BF16),
            pltpu.VMEM((2, n, nx, *block), BF16),
            pltpu.VMEM((nx, 2, *block), BF16),
            pltpu.VMEM((nx, 2, *block), BF16),
            pltpu.VMEM((2, *block), BF16),
            pltpu.VMEM((2, n, *block), BF16),
        ]
        + [dma(shape) for shape in sems],
        compiler_params=pltpu.CompilerParams(collective_id=0, has_side_effects=True, vmem_limit_bytes=24 << 20),
    )(*[pltpu.with_memory_space_constraint(v, pltpu.HBM) for v in args])


def finish(dtokens, sums, late):
    shape = jax.ShapeDtypeStruct
    shapes = ((ROWS, C), (PMAX, H), (H,), (PMAX, H), (PMAX,), (C,), (C,))
    return pl.pallas_call(
        finish_kernel,
        name="finish",
        out_shape=tuple(shape(s, BF16) for s in shapes),
        in_specs=[VMEM] * 3,
        out_specs=(HBM,) + (VMEM,) * 6,
        scratch_shapes=[pltpu.SemaphoreType.DMA],
        compiler_params=pltpu.CompilerParams(vmem_limit_bytes=10 << 20),
    )(dtokens, sums, late)


def solution(mesh):
    ny, nz = mesh.shape["dp"] // NX, mesh.shape["group"] // 2

    def local(*args):
        dtokens, sums, late = main(NX, ny, nz, *args)
        dtokens, w_in, b_in, w_out, b_out, gain, shift = finish(
            dtokens, sums.reshape(2, BLOCKS, LINES, 128), late
        )
        return (dtokens, w_in, b_in, w_out.T, b_out, gain, shift)

    rows = P(AXES, None)
    in_specs = (rows, rows, P(AXES)) + (P(),) * 7
    out_specs = (rows,) + (P(),) * 6
    return jax.shard_map(local, mesh=mesh, in_specs=in_specs, out_specs=out_specs, check_vma=False)
```

time: 45.7 us -> 43.7 us (0.956)
  Pallas kernels: 44.9 us -> 43 us
    pallas_call x1, Pallas kernels: 43.7 us -> 41.4 us  [main(): pl.pallas_call(lambda *refs: main_kernel(nx, ny, nz, *refs), name='main',...]
where the time goes in v3:
time: 43.7 us; the launch traced here: 43.6 us
  Pallas kernels  43 us (98%)
  between operations  0.64 us (1%)
    pallas_call x1, Pallas kernels, main(): pl.pallas_call(lambda *refs: main_kernel(nx, ny, nz, *refs), name='main',...  41.4 us
    pallas_call x1, Pallas kernels, finish(): pl.pallas_call(finish_kernel, name='finish', out_shape=tuple((shape(s, BF...  1.58 us

profile of v3, /device:TPU:1, one launch (start us, length us, event | category | flops | bytes accessed | tf_op | source)
XLA Modules:
  0.0 43.6 jit_solution(17236301974585691904)
XLA Ops:
  0.6 41.4 %main.1 = (bf16[320,768]{1,0:T(8,128)(2,1)S(1)}, bf16[2,2,8,4,16,128]{5,4,3,2,1,0:T(8,128)(2,1)S(1)}, bf16[16,128]{1,0:T(8,128)(2,1)S(1)}) custom-call(s32[3,512]{1,0:T(4,128)} %bitcast.7, s32[3,512]{1,0:T(4,128)} %bitcast.8, bf16[320,768]{1,0:T(8,128)(2,1)} %refs_2_.1, bf16[320,768]{1,0:T(8,128)(2,1)} %refs_3_.1, s32[320]{0:T(512)} %refs_4_.1, ...), custom_call_target="tpu_custom_call" | custom-call | tf_op jit(solution)/shard_map/main/pallas_call | solution.py:423
  42.0 1.6 %finish.1 = (bf16[320,768]{1,0:T(8,128)(2,1)}, bf16[288,384]{1,0:T(8,128)(2,1)}, bf16[384]{0:T(512)(128)(2,1)}, bf16[288,384]{1,0:T(8,128)(2,1)}, bf16[288]{0:T(...) custom-call(bf16[320,768]{1,0:T(8,128)(2,1)S(1)} %get-tuple-element.17.dtok_ref, ...), custom_call_target="tpu_custom_call" | custom-call | tf_op jit(solution)/shard_map/finish/pallas_call | solution.py:485

commit v4 on v3

--- a/solution.py
+++ b/solution.py
@@ -356,20 +356,14 @@
             send(block, block, s4.at[k], v4.at[k], x_peer(d))
     bl_ref[3] = late_wait(2)
     late_send(3)
-    sixth = {}
     for k in (0, 1):
         drain(out_ref.at[k, c, mine[k], pl.ds(0, nx - 1)], v4.at[k])
         block = out_ref.at[k, c, mine[k]]
         for d in rings[k]:
-            sixth[k, d] = send(block, block, s5.at[k], v5.at[k, d], peers[k](d))
-        send(block, block, s6.at[k], v6.at[k], partner)
-    for i in range(max(chip) - 1):
-        for k in (0, 1):
-            if i < chip[k] - 1:
-                d = rings[k][i]
-                sixth[k, d].wait_recv()
-                block = out_ref.at[k, c, back(mine[k], d, chip[k])]
-                send(block, block, s6.at[k], v6.at[k], partner)
+            send(block, block, s5.at[k], v5.at[k], peers[k](d))
+    for k in (0, 1):
+        drain(q.at[k, rest[k]], v5.at[k])
+        send(out_ref.at[k, c], out_ref.at[k, c], s6.at[k], v6.at[k], partner)
     late_out[...] = late_wait(3)
     for k in (0, 1):
         drain(out_ref.at[k, mate], v6.at[k])
@@ -384,9 +378,8 @@
         drain(slots.at[pl.ds(0, n - 1)], sl.at[stage])
 
 
-def finish_kernel(dtok_ref, sum_ref, late_ref, out_ref, wi_ref, bi_ref, wo_ref, bo_ref, gain_ref, shift_ref, sem):
-    move = pltpu.make_async_copy(dtok_ref, out_ref, sem)
-    move.start()
+def finish_kernel(dtok_ref, sum_ref, late_ref, out_ref, wi_ref, bi_ref, wo_ref, bo_ref, gain_ref, shift_ref):
+    out_ref[...] = dtok_ref[...]
     one = late_ref[...].astype(F32)
     total = one * one
     for k in (0, 1):
@@ -410,7 +403,6 @@
         width = min(128, PMAX - b * 128)
         bi_ref[pl.ds(b * 128, 128)] = two[b].astype(BF16)
         bo_ref[pl.ds(b * 128, width)] = two[3 + b, :width].astype(BF16)
-    move.wait()
 
 
 def main(nx, ny, nz, tokens, cotangent, patch_mask, image_tiles, patches, *weights):
@@ -419,7 +411,7 @@
     n, places = max(ny, nz), image_tiles.shape[0]
     shape, dma = jax.ShapeDtypeStruct, pltpu.SemaphoreType.DMA
     block = (BLOCKS // (2 * n * nx) * LINES, 128)
-    sems = [(2,), (2, n), (2,), (2,), (1,), (1,), (2,), (2,), (2,), (2,), (2,), (2, n), (2,), (2,)]
+    sems = [(2,), (2, n), (2,), (2,), (1,), (1,), (2,), (2,), (2,), (2,), (2,), (2,), (2,), (2,)]
     return pl.pallas_call(
         lambda *refs: main_kernel(nx, ny, nz, *refs),
         name="main",
@@ -487,8 +479,7 @@
         name="finish",
         out_shape=tuple(shape(s, BF16) for s in shapes),
         in_specs=[VMEM] * 3,
-        out_specs=(HBM,) + (VMEM,) * 6,
-        scratch_shapes=[pltpu.SemaphoreType.DMA],
+        out_specs=(VMEM,) * 7,
         compiler_params=pltpu.CompilerParams(vmem_limit_bytes=10 << 20),
     )(dtokens, sums, late)
 

time: 43.7 us -> 43.3 us (level)
    pallas_call x1, Pallas kernels: 1.58 us -> 1.14 us  [finish(): pl.pallas_call(finish_kernel, name='finish', out_shape=tuple((shape(s, BF...]
where the time goes in v4:
time: 43.3 us; the launch traced here: 43.2 us
  Pallas kernels  42.6 us (98%)
  between operations  0.64 us (1%)
    pallas_call x1, Pallas kernels, main(): pl.pallas_call(lambda *refs: main_kernel(nx, ny, nz, *refs), name='main',...  41.4 us
    pallas_call x1, Pallas kernels, finish(): pl.pallas_call(finish_kernel, name='finish', out_shape=tuple((shape(s, BF...  1.14 us

profile of v4, /device:TPU:1, one launch (start us, length us, event | category | flops | bytes accessed | tf_op | source)
XLA Modules:
  0.0 43.2 jit_solution(990084346167709842)
XLA Ops:
  0.6 41.4 %main.1 = (bf16[320,768]{1,0:T(8,128)(2,1)S(1)}, bf16[2,2,8,4,16,128]{5,4,3,2,1,0:T(8,128)(2,1)S(1)}, bf16[16,128]{1,0:T(8,128)(2,1)S(1)}) custom-call(s32[3,512]{1,0:T(4,128)} %bitcast.7, s32[3,512]{1,0:T(4,128)} %bitcast.8, bf16[320,768]{1,0:T(8,128)(2,1)} %refs_2_.1, bf16[320,768]{1,0:T(8,128)(2,1)} %refs_3_.1, s32[320]{0:T(512)} %refs_4_.1, ...), custom_call_target="tpu_custom_call" | custom-call | tf_op jit(solution)/shard_map/main/pallas_call | solution.py:415
  42.1 1.1 %finish.1 = (bf16[320,768]{1,0:T(8,128)(2,1)}, bf16[288,384]{1,0:T(8,128)(2,1)}, bf16[384]{0:T(512)(128)(2,1)}, bf16[288,384]{1,0:T(8,128)(2,1)}, bf16[288]{0:T(...) custom-call(bf16[320,768]{1,0:T(8,128)(2,1)S(1)} %get-tuple-element.17.dtok_ref, ...), custom_call_target="tpu_custom_call" | custom-call | tf_op jit(solution)/shard_map/finish/pallas_call | solution.py:477

commit v5 on v4

--- a/solution.py
+++ b/solution.py
@@ -80,7 +80,6 @@
     x_ref[TILES:] = jnp.zeros((PMAX // TILE, TILE, C), BF16)
     d_ref[TILES:] = jnp.zeros((PMAX // TILE, TILE, C), BF16)
     sum_ref[...] = jnp.zeros((H, 128), F32)
-    ro_ref[TILES:] = jnp.zeros((PMAX // TILE, TILE, 128), F32)
     small_ref[...] = jnp.zeros((LINES, 128), F32)
     late_ref[...] = jnp.zeros((LINES, 128), F32)
     for load in loads[:6]:
@@ -105,34 +104,27 @@
         x_ref[t] = ((normal * gain + shift) * wide(alive_ref[rows, :])).astype(BF16)
     for load in loads[6:]:
         load.wait()
-    for t in range(TILES):
-        rows = slice(t * TILE, (t + 1) * TILE)
-        dout = (cot_ref[rows, :].astype(F32) * wide(alive_ref[rows, :])).astype(BF16)
-        d_ref[t] = dout
-        ro_ref[t] = jnp.broadcast_to(jnp.sum(dout.astype(F32), axis=1, keepdims=True), (TILE, 128))
 
     bias = column(bi_ref[...].reshape(1, H))
     bias = jnp.concatenate([bias, bias], axis=1)
     wt_ref[0] = jnp.transpose(wi_ref[...])
     wt_ref[1] = jnp.transpose(wo_ref[...])
-    bo_ref[...] = jnp.zeros((H, 128), F32)
-
-    def place_rows(j):
+
+    def place_rows(j, source, target):
         tiles, start, _ = images[j]
         for u in range(SPANS[j] // TILE):
-            held = jnp.where(u < tiles, 1.0, 0.0)
-            keep = held.astype(BF16)
-            bo_ref[u * TILE : (u + 1) * TILE, :] += ro_ref[start + u] * held
-            at = slice((BASES[j] + u) * TILE, (BASES[j] + u + 1) * TILE)
-            xs_ref[at, :] = x_ref[start + u] * keep
-            ds_ref[at, :] = d_ref[start + u] * keep
+            keep = jnp.where(u < tiles, 1.0, 0.0).astype(BF16)
+            target[(BASES[j] + u) * TILE : (BASES[j] + u + 1) * TILE, :] = source[start + u] * keep
 
     def own(j):
         return slice(BASES[j] * TILE, BASES[j] * TILE + SPANS[j])
 
-    def project(j, part):
+    def project_pre(j, part):
         cols = slice(part * 256, (part + 1) * 256)
         pre_ref[j % 2, :, cols] = dot(wt_ref[0, :, : SPANS[j]], xs_ref[own(j), cols], 1, 0)
+
+    def project_dz(j, part):
+        cols = slice(part * 256, (part + 1) * 256)
         dz_ref[j % 2, :, cols] = dot(wt_ref[1, :, : SPANS[j]], ds_ref[own(j), cols], 1, 0)
 
     def activate(j, part):
@@ -153,11 +145,20 @@
             go_ref[:span, :] = go if j == 0 else go_ref[:span, :] + go
 
     for j in range(3):
-        place_rows(j)
+        place_rows(j, x_ref, xs_ref)
+    for part in range(3):
+        project_pre(0, part)
+    for t in range(TILES):
+        rows = slice(t * TILE, (t + 1) * TILE)
+        d_ref[t] = (cot_ref[rows, :].astype(F32) * wide(alive_ref[rows, :])).astype(BF16)
+    for j in range(3):
+        place_rows(j, d_ref, ds_ref)
     for step in range(5):
         for part in range(3):
+            if 0 < step < 3:
+                project_pre(step, part)
             if step < 3:
-                project(step, part)
+                project_dz(step, part)
             if 1 <= step < 4:
                 activate(step - 1, part)
             if step >= 2:
@@ -165,7 +166,6 @@
 
     for b in range(3):
         small_ref[b : b + 1, :] = jnp.sum(jnp.transpose(sum_ref[b * 128 : (b + 1) * 128, :]), axis=0, keepdims=True)
-        small_ref[3 + b : 4 + b, :] = jnp.transpose(bo_ref[b * 128 : (b + 1) * 128, :])[0:1]
     n, nx, lines = pack_ref.shape[2:5]
     each = lines // LINES
 
@@ -185,7 +185,16 @@
     return images
 
 
-def late_sums(images, wi_ref, dpre_ref, dn_ref, nx_ref, alive_ref, late_ref, bl_ref):
+def late_sums(images, wi_ref, dpre_ref, dn_ref, nx_ref, alive_ref, late_ref, bl_ref, d_ref, ro_ref, bo_ref):
+    ro_ref[TILES:] = jnp.zeros((PMAX // TILE, TILE, 128), F32)
+    bo_ref[...] = jnp.zeros((H, 128), F32)
+    for t in range(TILES):
+        ro_ref[t] = jnp.broadcast_to(jnp.sum(d_ref[t].astype(F32), axis=1, keepdims=True), (TILE, 128))
+    for j, (tiles, start, _) in enumerate(images):
+        for u in range(SPANS[j] // TILE):
+            bo_ref[u * TILE : (u + 1) * TILE, :] += ro_ref[start + u] * jnp.where(u < tiles, 1.0, 0.0)
+    for b in range(3):
+        late_ref[12 + b : 13 + b, :] = jnp.transpose(bo_ref[b * 128 : (b + 1) * 128, :])[0:1]
     for j in range(3):
         back_rows = dot(wi_ref[: SPANS[j], :], dpre_ref[j], 1, 0).astype(BF16)
         for u in range(SPANS[j] // TILE):
@@ -321,7 +330,7 @@
         q[k, at] = (pack_ref[k, c, at].astype(F32) + r0[k, at].astype(F32)).astype(BF16)
         if d:
             send(q.at[k, at], r1.at[k, mine[k]], s1.at[k], v1.at[k], peers[k](d))
-    late_sums(images, wi_ref, dpre_ref, dn_ref, nx_ref, alive_ref, late_ref, bl_ref.at[0])
+    late_sums(images, wi_ref, dpre_ref, dn_ref, nx_ref, alive_ref, late_ref, bl_ref.at[0], d_ref, ro_ref, bo_ref)
     late_send(0)
     token_gradient(images, cot_ref, gain_ref, dtok_ref, nx_ref, inv_ref, alive_ref, dn_ref)
     for k in (0, 1):
@@ -359,7 +368,7 @@
     for k in (0, 1):
         drain(out_ref.at[k, c, mine[k], pl.ds(0, nx - 1)], v4.at[k])
         block = out_ref.at[k, c, mine[k]]
-        for d in rings[k]:
+        for d in rings[k][::-1]:
             send(block, block, s5.at[k], v5.at[k], peers[k](d))
     for k in (0, 1):
         drain(q.at[k, rest[k]], v5.at[k])
@@ -402,7 +411,7 @@
     for b in range(3):
         width = min(128, PMAX - b * 128)
         bi_ref[pl.ds(b * 128, 128)] = two[b].astype(BF16)
-        bo_ref[pl.ds(b * 128, width)] = two[3 + b, :width].astype(BF16)
+        bo_ref[pl.ds(b * 128, width)] = one[12 + b, :width].astype(BF16)
 
 
 def main(nx, ny, nz, tokens, cotangent, patch_mask, image_tiles, patches, *weights):

time: 43.3 us -> 43.1 us (level)
  no operation moved by 1% of the time
where the time goes in v5:
time: 43.1 us; the launch traced here: 43 us
  Pallas kernels  42.3 us (98%)
  between operations  0.64 us (1%)
    pallas_call x1, Pallas kernels, main(): pl.pallas_call(lambda *refs: main_kernel(nx, ny, nz, *refs), name='main',...  41.2 us
    pallas_call x1, Pallas kernels, finish(): pl.pallas_call(finish_kernel, name='finish', out_shape=tuple((shape(s, BF...  1.14 us

profile of v5, /device:TPU:1, one launch (start us, length us, event | category | flops | bytes accessed | tf_op | source)
XLA Modules:
  0.0 43.0 jit_solution(3962345379376015634)
XLA Ops:
  0.6 41.2 %main.1 = (bf16[320,768]{1,0:T(8,128)(2,1)S(1)}, bf16[2,2,8,4,16,128]{5,4,3,2,1,0:T(8,128)(2,1)S(1)}, bf16[16,128]{1,0:T(8,128)(2,1)S(1)}) custom-call(s32[3,512]{1,0:T(4,128)} %bitcast.7, s32[3,512]{1,0:T(4,128)} %bitcast.8, bf16[320,768]{1,0:T(8,128)(2,1)} %refs_2_.1, bf16[320,768]{1,0:T(8,128)(2,1)} %refs_3_.1, s32[320]{0:T(512)} %refs_4_.1, ...), custom_call_target="tpu_custom_call" | custom-call | tf_op jit(solution)/shard_map/main/pallas_call | solution.py:424
  41.8 1.1 %finish.1 = (bf16[320,768]{1,0:T(8,128)(2,1)}, bf16[288,384]{1,0:T(8,128)(2,1)}, bf16[384]{0:T(512)(128)(2,1)}, bf16[288,384]{1,0:T(8,128)(2,1)}, bf16[288]{0:T(...) custom-call(bf16[320,768]{1,0:T(8,128)(2,1)S(1)} %get-tuple-element.17.dtok_ref, ...), custom_call_target="tpu_custom_call" | custom-call | tf_op jit(solution)/shard_map/finish/pallas_call | solution.py:486
